TPU v7x, 32 devices: a whole 2x2x4 slice. The times are simulated.
32 devices in a mesh: gx: 8 (over z, x), gy: 4 (over y, core).
Axes of the slice: x: 2, y: 2, z: 4, core: 2. Of those that a mesh axis runs over, the one named last changes fastest.
Arguments:
- u_prev: float32 [3, 32, 128, 2048], P(None, None, 'gx', 'gy'), may hold values from -6 to 6
- u_now: float32 [3, 32, 128, 2048], P(None, None, 'gx', 'gy'), may hold values from -6 to 6
- speeds: float32 [2, 32, 128, 2048], P(None, None, 'gx', 'gy'), may hold values from 0.1 to 0.24
- sites: int32 [12288], P(('gx', 'gy')), may hold values from 0 to 8191
- routes: int32 [12288, 1], P(('gx', 'gy')), may hold values from 0 to 31; in each aligned block of 384 rows (0 to 383, 384 to 767, ...) at most 32 rows name the same one
- frame_disp: float32 [240, 32768], P(None, ('gx', 'gy')), may hold values from -4 to 4
- frame_vel: float32 [240, 32768], P(None, ('gx', 'gy')), may hold values from -6 to 6
- frame_acc: float32 [240, 32768], P(None, ('gx', 'gy')), may hold values from -6 to 6
- frame_hyst: float32 [240, 32768], P(None, ('gx', 'gy')), may hold values from -0.5 to 0.5
- frame_kind: int32 [32768], P(('gx', 'gy')), may hold values from 0 to 3
- stiffness: float32 [4, 240, 240], replicated, as said below
Outputs:
- field_before: float32 [3, 32, 128, 2048], P(None, None, 'gx', 'gy')
- field_last: float32 [3, 32, 128, 2048], P(None, None, 'gx', 'gy')
- disp_next: float32 [240, 32768], P(None, ('gx', 'gy'))
- vel_next: float32 [240, 32768], P(None, ('gx', 'gy'))
- acc_next: float32 [240, 32768], P(None, ('gx', 'gy'))
- hyst_next: float32 [240, 32768], P(None, ('gx', 'gy'))
Inputs may be any that keep to these rules, and one draw needn't show every extreme that they name: `routes`: among the buildings of one device, no owner is named by more than 32 of them, a bound that some block reaches. `stiffness`: diagonal entries between 1 and 2; off-diagonal entries small.
All inputs are finite; a program needn't handle non-finite values.
Results may differ from a plain program's by a relative error of at most 0.00023.
Values sent between devices are 32-bit elements; how exact they have to be, the bound alone decides.
A program may use at most 192 MiB of HBM per device.

v0:
```python
import jax
import jax.numpy as jnp
from jax import lax
from jax.sharding import PartitionSpec as P

STEPS = 4


time_step = 0.5
damping = 0.1
yield_drift = 0.5
hyst_stiff = 1.0
ground_gain = 0.1


def with_halo(cells, sides, width):
    for axis, dim in sides:
        count = lax.axis_size(axis)
        ends = count - 1
        head = lax.slice_in_dim(cells, 0, width, axis=dim)
        tail = lax.slice_in_dim(cells, cells.shape[dim] - width, cells.shape[dim], axis=dim)
        cells = jnp.concatenate(
            [
                lax.ppermute(tail, axis, [(i, (i + 1) % count) for i in range(ends)]),
                cells,
                lax.ppermute(head, axis, [((i + 1) % count, i) for i in range(ends)]),
            ],
            axis=dim,
        )
    return cells


def trim_rim(array, dims, width):
    for dim in dims:
        array = lax.slice_in_dim(array, width, array.shape[dim] - width, axis=dim)
    return array


def second_diff(padded, dim):
    length = padded.shape[dim]

    def part(start):
        return lax.slice_in_dim(padded, start, length - 4 + start, axis=dim)

    return (16.0 * (part(1) + part(3)) - (part(0) + part(4)) - 30.0 * part(2)) / 12.0


def wave_accel(padded, speeds):
    along_depth = trim_rim(second_diff(padded, 1), (2, 3), 2)
    along_east = trim_rim(second_diff(padded, 2), (1, 3), 2)
    along_north = trim_rim(second_diff(padded, 3), (1, 2), 2)
    own_term = jnp.stack([along_east[0], along_north[1], along_depth[2]])
    total = along_east + along_north + along_depth
    return speeds[0] * own_term + speeds[1] * (total - own_term)


def depth_pad(field):
    return jnp.pad(field, ((0, 0), (2, 2), (0, 0), (0, 0)))


def shift_down(values):
    return jnp.concatenate([jnp.zeros_like(values[:3]), values[:-3]], axis=0)


def shift_up(values):
    return jnp.concatenate([values[3:], jnp.zeros_like(values[:3])], axis=0)


def shards(
    u_prev,
    u_now,
    speeds,
    sites,
    routes,
    frame_disp,
    frame_vel,
    frame_acc,
    frame_hyst,
    frame_kind,
    stiffness,
):
    tile_x = u_now.shape[2]
    tile_y = u_now.shape[3]
    older = u_prev
    newer = u_now
    history = []
    for step in range(STEPS):
        padded = with_halo(newer, (("gx", 2), ("gy", 3)), 2)
        nxt = 2.0 * newer - older + wave_accel(depth_pad(padded), speeds)
        older = newer
        newer = nxt
        history.append(nxt)
    level_last = history[-1]
    level_before = history[-2]
    level_third = history[-3]
    surface = ground_gain * (level_last - 2.0 * level_before + level_third)[:, 0]
    surface = surface.reshape(3, tile_x * tile_y)
    motion = jnp.take(surface, sites, axis=1)
    devices = lax.axis_size("gx") * lax.axis_size("gy")
    rows_dev = frame_kind.shape[0]
    capacity = rows_dev // devices
    count = sites.shape[0]
    target_dev = routes[:, 0]
    onehot = (target_dev[:, None] == jnp.arange(devices, dtype=jnp.int32)[None, :]).astype(
        jnp.float32
    )
    row_ids = jnp.arange(count, dtype=jnp.int32)
    lower = (row_ids[:, None] > row_ids[None, :]).astype(jnp.float32)
    before = jnp.dot(lower, onehot, precision=lax.Precision.HIGHEST)
    rank = jnp.sum(before * onehot, axis=1).astype(jnp.int32)
    slot = target_dev * capacity + rank
    placing = (slot[:, None] == jnp.arange(rows_dev, dtype=jnp.int32)[None, :]).astype(jnp.float32)
    outgoing = jnp.dot(motion, placing, precision=lax.Precision.HIGHEST)
    arrived = lax.all_to_all(
        outgoing.reshape(3, devices, capacity),
        ("gx", "gy"),
        split_axis=1,
        concat_axis=1,
        tiled=True,
    )
    slot_motion = arrived.reshape(3, rows_dev)
    disp_next = frame_disp + time_step * frame_vel + 0.5 * time_step * time_step * frame_acc
    drift_change = disp_next - shift_down(disp_next) - (frame_disp - shift_down(frame_disp))
    hyst_next = jnp.clip(frame_hyst + drift_change, -yield_drift, yield_drift)
    elastic = jnp.zeros_like(disp_next)
    for kind in range(stiffness.shape[0]):
        product = jnp.dot(stiffness[kind], disp_next, precision=lax.Precision.HIGHEST)
        elastic = elastic + jnp.where(frame_kind[None, :] == kind, product, 0.0)
    forcing = jnp.tile(slot_motion, (frame_disp.shape[0] // 3, 1))
    acc_next = (
        -forcing
        - damping * (frame_vel + 0.5 * time_step * frame_acc)
        - elastic
        - hyst_stiff * (hyst_next - shift_up(hyst_next))
    )
    vel_next = frame_vel + 0.5 * time_step * (frame_acc + acc_next)
    return (level_before, level_last, disp_next, vel_next, acc_next, hyst_next)


def solution(mesh):
    placed = (
        P(None, None, "gx", "gy"),
        P(None, None, "gx", "gy"),
        P(None, None, "gx", "gy"),
        P(("gx", "gy")),
        P(("gx", "gy"), None),
        P(None, ("gx", "gy")),
        P(None, ("gx", "gy")),
        P(None, ("gx", "gy")),
        P(None, ("gx", "gy")),
        P(("gx", "gy")),
        P(),
    )
    return jax.shard_map(
        shards,
        mesh=mesh,
        in_specs=placed,
        out_specs=(
            P(None, None, "gx", "gy"),
            P(None, None, "gx", "gy"),
            P(None, ("gx", "gy")),
            P(None, ("gx", "gy")),
            P(None, ("gx", "gy")),
            P(None, ("gx", "gy")),
        ),
        check_vma=False,
    )
```

profile of v0, /device:TPU:0, one launch (start us, length us, event | category | flops | bytes accessed | tf_op | source)
XLA Modules:
  0.0 308.9 jit_solution(1339917139413191721)
XLA Ops:
  4.5 5.5 %collective-permute-start = (f32[3,32,2,512]{3,1,2,0:T(8,128)S(1)}, f32[3,32,2,512]{3,1,2,0:T(8,128)S(1)}, u32[]{:S(2)}, u32[]{:S(2)}) collective-permute-start(f32[3,32,2,512]{3,1,2,0:T(8,128)S(1)} %copy.227), channel_id=1, source_target_pairs={{0,4},{4,8},{8,12},{12,16},{16,20},{20,24},{24,28},{1,5},{5,9},{9,... | collective-permute-start | bytes 1179656 | tf_op jit(solution)/shard_map/ppermute | solution.py:24
  13.1 4.0 %collective-permute-done.1 = f32[3,32,2,512]{3,1,2,0:T(8,128)S(1)} collective-permute-done((f32[3,32,2,512]{3,1,2,0:T(8,128)S(1)}, f32[3,32,2,512]{3,1,2,0:T(8,128)S(1)}, u32[]{:S(2)}, u32[]{:S(2)}) %collective-permute-start.1) | collective-permute-done | bytes 393248 | tf_op jit(solution)/shard_map/ppermute | solution.py:26
  17.4 8.3 %collective-permute-done = f32[3,32,2,512]{3,1,2,0:T(8,128)S(1)} collective-permute-done((f32[3,32,2,512]{3,1,2,0:T(8,128)S(1)}, f32[3,32,2,512]{3,1,2,0:T(8,128)S(1)}, u32[]{:S(2)}, u32[]{:S(2)}) %collective-permute-start) | collective-permute-done | bytes 393248 | tf_op jit(solution)/shard_map/ppermute | solution.py:24
  34.9 3.8 %collective-permute-start.2 = (f32[3,32,20,2]{1,2,3,0:T(8,128)}, f32[3,32,20,2]{1,2,3,0:T(8,128)}, u32[]{:S(2)}, u32[]{:S(2)}) collective-permute-start(f32[3,32,20,2]{1,2,3,0:T(8,128)} %copy.195), channel_id=1, source_target_pairs={{0,1},{1,2},{2,3},{4,5},{5,6},{6,7},{8,9},{9,10},{10,11},{12,13},{... | collective-permute-start | bytes 46088 | tf_op jit(solution)/shard_map/ppermute | solution.py:24
  46.7 5.8 %pad_maximum_fusion = f32[3,32,20,516]{3,2,1,0:T(8,128)S(1)} fusion(f32[3,32,20,2]{3,2,1,0:T(8,128)} %copy.198, f32[3,32,2,512]{3,2,1,0:T(2,128)S(1)} %copy.194, f32[3,32,16,512]{3,2,1,0:T(8,128)S(1)} %copy-done.5, f32[3,32,2,512]{3,2,1,0:T(2,128)} %copy-done.23, f32[3,32,20,2]{3,2,1,0:T(8,128)} %copy.197), kind=kLoop, calls=%fused_computation.81 | loop fusion | flops 3962880 | bytes 7925760 | tf_op jit(solution)/shard_map/concatenate | solution.py:22
  55.0 5.2 %fusion.28 = f32[3,36,20,512]{3,2,1,0:T(8,128)S(1)} fusion(f32[3,32,20,516]{3,2,1,0:T(8,128)S(1)} %pad_maximum_fusion), kind=kLoop, calls=%fused_computation.89 | loop fusion | flops 7741440 | bytes 8386560 | tf_op jit(solution)/shard_map/div | solution.py:45
  60.2 3.8 %fusion.56 = f32[3,36,16,516]{3,2,1,0:T(8,128)} fusion(f32[3,32,20,516]{3,2,1,0:T(8,128)S(1)} %pad_maximum_fusion), kind=kLoop, calls=%fused_computation.117 | loop fusion | flops 6241536 | bytes 7529472 | tf_op jit(solution)/shard_map/div | solution.py:45
  66.9 5.2 %fusion.95 = f32[3,32,16,512]{3,2,1,0:T(8,128)S(1)} fusion(f32[3,32,20,516]{3,2,1,0:T(8,128)S(1)} %fusion.4, f32[3,36,20,512]{3,2,1,0:T(8,128)S(1)} %fusion.28, f32[3,36,16,516]{3,2,1,0:T(8,128)} %fusion.56, f32[1,32,16,512]{3,2,1,0:T(8,128)S(1)} %slice.474, f32[1,32,16,512]{3,2,1,0:T(8,128)S(1)} %slice.473, f32[1,32,16,512]{3,2,1,0:T(8,128)S(1)} %slice.472, ...), kind=kLoop, calls=%fused_computation.163 | loop fusion | flops 8650752 | bytes 24117248 | tf_op jit(solution)/shard_map/add | solution.py:89
  74.0 5.4 %collective-permute-start.4 = (f32[3,32,2,512]{3,1,2,0:T(8,128)S(1)}, f32[3,32,2,512]{3,1,2,0:T(8,128)S(1)}, u32[]{:S(2)}, u32[]{:S(2)}) collective-permute-start(f32[3,32,2,512]{3,1,2,0:T(8,128)S(1)} %copy.199), channel_id=1, source_target_pairs={{0,4},{4,8},{8,12},{12,16},{16,20},{20,24},{24,28},{1,5},{5,9},{9,... | collective-permute-start | bytes 1179656 | tf_op jit(solution)/shard_map/ppermute | solution.py:24
  83.0 3.9 %collective-permute-done.5 = f32[3,32,2,512]{3,1,2,0:T(8,128)S(1)} collective-permute-done((f32[3,32,2,512]{3,1,2,0:T(8,128)S(1)}, f32[3,32,2,512]{3,1,2,0:T(8,128)S(1)}, u32[]{:S(2)}, u32[]{:S(2)}) %collective-permute-start.5) | collective-permute-done | bytes 393248 | tf_op jit(solution)/shard_map/ppermute | solution.py:26
  87.2 8.3 %collective-permute-done.4 = f32[3,32,2,512]{3,1,2,0:T(8,128)S(1)} collective-permute-done((f32[3,32,2,512]{3,1,2,0:T(8,128)S(1)}, f32[3,32,2,512]{3,1,2,0:T(8,128)S(1)}, u32[]{:S(2)}, u32[]{:S(2)}) %collective-permute-start.4) | collective-permute-done | bytes 393248 | tf_op jit(solution)/shard_map/ppermute | solution.py:24
  113.3 5.8 %pad_maximum_fusion.1 = f32[3,32,20,516]{3,2,1,0:T(8,128)S(1)} fusion(f32[3,32,20,2]{3,2,1,0:T(8,128)} %copy.206, f32[3,32,2,512]{3,2,1,0:T(2,128)S(1)} %copy.202, f32[3,32,16,512]{3,2,1,0:T(8,128)S(1)} %fusion.95, f32[3,32,2,512]{3,2,1,0:T(2,128)} %copy-done.25, f32[3,32,20,2]{3,2,1,0:T(8,128)} %copy.205), kind=kLoop, calls=%fused_computation.82 | loop fusion | flops 3962880 | bytes 7925760 | tf_op jit(solution)/shard_map/concatenate | solution.py:22
  121.6 5.2 %fusion.35 = f32[3,36,20,512]{3,2,1,0:T(8,128)S(1)} fusion(f32[3,32,20,516]{3,2,1,0:T(8,128)S(1)} %pad_maximum_fusion.1), kind=kLoop, calls=%fused_computation.96 | loop fusion | flops 7741440 | bytes 8386560 | tf_op jit(solution)/shard_map/div | solution.py:45
  126.9 3.8 %fusion.63 = f32[3,36,16,516]{3,2,1,0:T(8,128)} fusion(f32[3,32,20,516]{3,2,1,0:T(8,128)S(1)} %pad_maximum_fusion.1), kind=kLoop, calls=%fused_computation.124 | loop fusion | flops 6241536 | bytes 7529472 | tf_op jit(solution)/shard_map/div | solution.py:45
  134.0 5.4 %fusion.91 = f32[3,32,16,512]{3,2,1,0:T(8,128)S(1)} fusion(f32[3,32,20,516]{3,2,1,0:T(8,128)S(1)} %fusion.10, f32[3,36,20,512]{3,2,1,0:T(8,128)} %copy-done.19, f32[3,36,16,516]{3,2,1,0:T(8,128)} %fusion.63, f32[1,32,16,512]{3,2,1,0:T(8,128)S(1)} %slice.482, f32[1,32,16,512]{3,2,1,0:T(8,128)S(1)} %slice.481, f32[1,32,16,512]{3,2,1,0:T(8,128)S(1)} %slice.480, ...), kind=kLoop, calls=%fused_computation.157 | loop fusion | flops 8650752 | bytes 24117248 | tf_op jit(solution)/shard_map/add | solution.py:89
  142.0 5.9 %collective-permute-start.8 = (f32[3,32,2,512]{3,1,2,0:T(8,128)}, f32[3,32,2,512]{3,1,2,0:T(8,128)}, u32[]{:S(2)}, u32[]{:S(2)}) collective-permute-start(f32[3,32,2,512]{3,1,2,0:T(8,128)} %copy.207), channel_id=1, source_target_pairs={{0,4},{4,8},{8,12},{12,16},{16,20},{20,24},{24,28},{1,5},{5,9},{9,... | collective-permute-start | bytes 1179656 | tf_op jit(solution)/shard_map/ppermute | solution.py:24
  155.6 7.3 %collective-permute-done.8 = f32[3,32,2,512]{3,1,2,0:T(8,128)} collective-permute-done((f32[3,32,2,512]{3,1,2,0:T(8,128)}, f32[3,32,2,512]{3,1,2,0:T(8,128)}, u32[]{:S(2)}, u32[]{:S(2)}) %collective-permute-start.8) | collective-permute-done | bytes 393248 | tf_op jit(solution)/shard_map/ppermute | solution.py:24
  182.0 5.8 %pad_maximum_fusion.2 = f32[3,32,20,516]{3,2,1,0:T(8,128)S(1)} fusion(f32[3,32,20,2]{3,2,1,0:T(8,128)} %copy.214, f32[3,32,2,512]{3,2,1,0:T(2,128)S(1)} %copy.210, f32[3,32,16,512]{3,2,1,0:T(8,128)S(1)} %fusion.91, f32[3,32,2,512]{3,2,1,0:T(2,128)} %copy-done.22, f32[3,32,20,2]{3,2,1,0:T(8,128)} %copy.213), kind=kLoop, calls=%fused_computation.83 | loop fusion | flops 3962880 | bytes 7925760 | tf_op jit(solution)/shard_map/concatenate | solution.py:22
  190.3 6.5 %fusion.42 = f32[3,36,20,512]{3,2,1,0:T(8,128)} fusion(f32[3,32,20,516]{3,2,1,0:T(8,128)S(1)} %pad_maximum_fusion.2), kind=kLoop, calls=%fused_computation.103 | loop fusion | flops 7741440 | bytes 8386560 | tf_op jit(solution)/shard_map/div | solution.py:45
  196.8 3.8 %fusion.70 = f32[3,36,16,516]{3,2,1,0:T(8,128)} fusion(f32[3,32,20,516]{3,2,1,0:T(8,128)S(1)} %pad_maximum_fusion.2), kind=kLoop, calls=%fused_computation.131 | loop fusion | flops 6241536 | bytes 7529472 | tf_op jit(solution)/shard_map/div | solution.py:45
  205.4 6.8 %broadcast_multiply_fusion = (f32[3,32,16,512]{3,2,1,0:T(8,128)}, f32[3,32,16,512]{3,2,1,0:T(8,128)S(1)}) fusion(f32[3,32,20,516]{3,2,1,0:T(8,128)S(1)} %fusion.16, f32[3,36,20,512]{3,2,1,0:T(8,128)} %fusion.42, f32[3,36,16,516]{3,2,1,0:T(8,128)} %fusion.70, f32[32,16,512]{2,1,0:T(8,128)S(1)} %copy-done.17, f32[1,32,16,512]{3,2,1,0:T(8,128)S(1)} %slice.490, ...), kind=kLoop, calls=%fused_computation.170 | loop fusion | flops 9437184 | bytes 27262976 | tf_op jit(solution)/shard_map/mul | solution.py:89
  214.0 5.3 %collective-permute-start.12 = (f32[3,32,2,512]{3,1,2,0:T(8,128)S(1)}, f32[3,32,2,512]{3,1,2,0:T(8,128)S(1)}, u32[]{:S(2)}, u32[]{:S(2)}) collective-permute-start(f32[3,32,2,512]{3,1,2,0:T(8,128)S(1)} %copy.215), channel_id=1, source_target_pairs={{0,4},{4,8},{8,12},{12,16},{16,20},{20,24},{24,28},{1,5},{5,9},{9,... | collective-permute-start | bytes 1179656 | tf_op jit(solution)/shard_map/ppermute | solution.py:24
  222.6 4.4 %collective-permute-done.13 = f32[3,32,2,512]{3,1,2,0:T(8,128)S(1)} collective-permute-done((f32[3,32,2,512]{3,1,2,0:T(8,128)S(1)}, f32[3,32,2,512]{3,1,2,0:T(8,128)S(1)}, u32[]{:S(2)}, u32[]{:S(2)}) %collective-permute-start.13) | collective-permute-done | bytes 393248 | tf_op jit(solution)/shard_map/ppermute | solution.py:26
  227.3 8.3 %collective-permute-done.12 = f32[3,32,2,512]{3,1,2,0:T(8,128)S(1)} collective-permute-done((f32[3,32,2,512]{3,1,2,0:T(8,128)S(1)}, f32[3,32,2,512]{3,1,2,0:T(8,128)S(1)}, u32[]{:S(2)}, u32[]{:S(2)}) %collective-permute-start.12) | collective-permute-done | bytes 393248 | tf_op jit(solution)/shard_map/ppermute | solution.py:24
  244.2 3.7 %collective-permute-start.14 = (f32[3,32,20,2]{1,2,3,0:T(8,128)}, f32[3,32,20,2]{1,2,3,0:T(8,128)}, u32[]{:S(2)}, u32[]{:S(2)}) collective-permute-start(f32[3,32,20,2]{1,2,3,0:T(8,128)} %copy.219), channel_id=1, source_target_pairs={{0,1},{1,2},{2,3},{4,5},{5,6},{6,7},{8,9},{9,10},{10,11},{12,13},{... | collective-permute-start | bytes 46088 | tf_op jit(solution)/shard_map/ppermute | solution.py:24
  252.7 6.2 %pad_maximum_fusion.3 = f32[3,32,20,516]{3,2,1,0:T(8,128)S(1)} fusion(f32[3,32,20,2]{3,2,1,0:T(8,128)} %copy.222, f32[3,32,2,512]{3,2,1,0:T(2,128)S(1)} %copy.218, f32[3,32,16,512]{3,2,1,0:T(8,128)} %copy-done.3, f32[3,32,2,512]{3,2,1,0:T(2,128)} %copy-done.24, f32[3,32,20,2]{3,2,1,0:T(8,128)} %copy.221), kind=kLoop, calls=%fused_computation.84 | loop fusion | flops 3962880 | bytes 7925760 | tf_op jit(solution)/shard_map/concatenate | solution.py:22
  261.4 5.2 %fusion.49 = f32[3,36,20,512]{3,2,1,0:T(8,128)S(1)} fusion(f32[3,32,20,516]{3,2,1,0:T(8,128)S(1)} %pad_maximum_fusion.3), kind=kLoop, calls=%fused_computation.110 | loop fusion | flops 7741440 | bytes 8386560 | tf_op jit(solution)/shard_map/div | solution.py:45
  266.7 3.8 %fusion.77 = f32[3,36,16,516]{3,2,1,0:T(8,128)} fusion(f32[3,32,20,516]{3,2,1,0:T(8,128)S(1)} %pad_maximum_fusion.3), kind=kLoop, calls=%fused_computation.138 | loop fusion | flops 6241536 | bytes 7529472 | tf_op jit(solution)/shard_map/div | solution.py:45
  273.3 5.8 %fusion.83 = f32[3,32,16,512]{3,2,1,0:T(8,128)} fusion(f32[3,32,20,516]{3,2,1,0:T(8,128)S(1)} %fusion.22, f32[3,36,20,512]{3,2,1,0:T(8,128)S(1)} %fusion.49, f32[3,36,16,516]{3,2,1,0:T(8,128)} %fusion.77, f32[1,32,16,512]{3,2,1,0:T(8,128)S(1)} %slice.498, f32[1,32,16,512]{3,2,1,0:T(8,128)S(1)} %slice.497, f32[1,32,16,512]{3,2,1,0:T(8,128)S(1)} %slice.496, ...), kind=kLoop, calls=%fused_computation.145 | loop fusion | flops 8650752 | bytes 24117248 | tf_op jit(solution)/shard_map/add | solution.py:89
  287.5 6.8 %all-to-all-start = ((f32[3,32,32]{2,0,1:T(4,128)}), f32[3,32,32]{2,0,1:T(4,128)S(1)}, u32[]{:S(2)}, u32[]{:S(2)}) async-start(f32[3,32,32]{2,0,1:T(4,128)} %copy.224), calls=%async_computation | async-start | bytes 131072 | tf_op jit(solution)/shard_map/all_to_all | solution.py:114
  294.3 3.7 %fusion.101 = f32[1024,240]{0,1:T(8,128)} fusion(f32[1024,240]{0,1:T(8,128)} %fusion.102, f32[240,1024]{1,0:T(8,128)} %multiply_add_fusion.1, pred[1024]{0:T(1024)(128)(4,1)S(1)} %copy-done.28, f32[4,240,240]{2,1,0:T(8,128)} %param.21), kind=kOutput, calls=%fused_computation.178 | convolution fusion | flops 708280320 | bytes 3195904 | tf_op jit(solution)/shard_map/dot_general | solution.py:127
  303.6 5.1 %multiply_add_fusion = (f32[240,1024]{1,0:T(8,128)}, f32[240,1024]{1,0:T(8,128)}) fusion(f32[240,1024]{1,0:T(8,128)} %param.17, f32[240,1024]{1,0:T(8,128)} %param.18, f32[240,1024]{1,0:T(8,128)S(1)} %copy-done.20, f32[237,1024]{1,0:T(8,128)} %slice.506, f32[1024,240]{0,1:T(8,128)} %fusion.101, f32[240,1024]{1,0:T(8,128)S(1)} %copy-done.10, ...), kind=kOutput, calls=%fused_computation.198 | convolution fusion | flops 710737920 | bytes 9094144 | tf_op jit(solution)/shard_map/dot_general | solution.py:127
  (164 shorter events, 133.5 us)
Async XLA Ops:
  0.6 26.1 %copy-start.5 = (f32[3,32,16,512]{3,2,1,0:T(8,128)S(1)}, f32[3,32,16,512]{3,2,1,0:T(8,128)}, u32[]{:S(2)}) copy-start(f32[3,32,16,512]{3,2,1,0:T(8,128)} %param.12) | copy-start | bytes 9437188
  3.1 14.0 %collective-permute-start.1 = (f32[3,32,2,512]{3,1,2,0:T(8,128)S(1)}, f32[3,32,2,512]{3,1,2,0:T(8,128)S(1)}, u32[]{:S(2)}, u32[]{:S(2)}) collective-permute-start(f32[3,32,2,512]{3,1,2,0:T(8,128)S(1)} %copy.228), channel_id=1, source_target_pairs={{4,0},{8,4},{12,8},{16,12},{20,16},{24,20},{28,24},{5,1},{9,5},{13... | collective-permute-start | bytes 1179656 | tf_op jit(solution)/shard_map/ppermute | solution.py:26
  4.5 21.2 %collective-permute-start = (f32[3,32,2,512]{3,1,2,0:T(8,128)S(1)}, f32[3,32,2,512]{3,1,2,0:T(8,128)S(1)}, u32[]{:S(2)}, u32[]{:S(2)}) collective-permute-start(f32[3,32,2,512]{3,1,2,0:T(8,128)S(1)} %copy.227), channel_id=1, source_target_pairs={{0,4},{4,8},{8,12},{12,16},{16,20},{20,24},{24,28},{1,5},{5,9},{9,... | collective-permute-start | bytes 1179656 | tf_op jit(solution)/shard_map/ppermute | solution.py:24
  31.2 10.7 %collective-permute-start.3 = (f32[3,32,20,2]{1,2,3,0:T(8,128)}, f32[3,32,20,2]{1,2,3,0:T(8,128)}, u32[]{:S(2)}, u32[]{:S(2)}) collective-permute-start(f32[3,32,20,2]{1,2,3,0:T(8,128)} %copy.196), channel_id=1, source_target_pairs={{1,0},{2,1},{3,2},{5,4},{6,5},{7,6},{9,8},{10,9},{11,10},{13,12},{... | collective-permute-start | bytes 46088 | tf_op jit(solution)/shard_map/ppermute | solution.py:26
  34.9 9.4 %collective-permute-start.2 = (f32[3,32,20,2]{1,2,3,0:T(8,128)}, f32[3,32,20,2]{1,2,3,0:T(8,128)}, u32[]{:S(2)}, u32[]{:S(2)}) collective-permute-start(f32[3,32,20,2]{1,2,3,0:T(8,128)} %copy.195), channel_id=1, source_target_pairs={{0,1},{1,2},{2,3},{4,5},{5,6},{6,7},{8,9},{9,10},{10,11},{12,13},{... | collective-permute-start | bytes 46088 | tf_op jit(solution)/shard_map/ppermute | solution.py:24
  66.9 12.5 %copy-start.29 = (s32[1024]{0:T(1024)S(1)}, s32[1024]{0:T(1024)}, u32[]{:S(2)}) copy-start(s32[1024]{0:T(1024)} %param.20) | copy-start | bytes 12292
  66.9 13.2 %copy-start.8 = (f32[240,1024]{1,0:T(8,128)S(1)}, f32[240,1024]{1,0:T(8,128)}, u32[]{:S(2)}) copy-start(f32[240,1024]{1,0:T(8,128)} %multiply_add_fusion.1) | copy-start | bytes 2949124
  72.1 41.2 %copy-start = (f32[3,32,16,512]{3,2,1,0:T(8,128)}, f32[3,32,16,512]{3,2,1,0:T(8,128)S(1)}, u32[]{:S(2)}) copy-start(f32[3,32,16,512]{3,2,1,0:T(8,128)S(1)} %fusion.95) | copy-start | bytes 9437188
  72.6 14.3 %collective-permute-start.5 = (f32[3,32,2,512]{3,1,2,0:T(8,128)S(1)}, f32[3,32,2,512]{3,1,2,0:T(8,128)S(1)}, u32[]{:S(2)}, u32[]{:S(2)}) collective-permute-start(f32[3,32,2,512]{3,1,2,0:T(8,128)S(1)} %copy.200), channel_id=1, source_target_pairs={{4,0},{8,4},{12,8},{16,12},{20,16},{24,20},{28,24},{5,1},{9,5},{13... | collective-permute-start | bytes 1179656 | tf_op jit(solution)/shard_map/ppermute | solution.py:26
  74.0 21.5 %collective-permute-start.4 = (f32[3,32,2,512]{3,1,2,0:T(8,128)S(1)}, f32[3,32,2,512]{3,1,2,0:T(8,128)S(1)}, u32[]{:S(2)}, u32[]{:S(2)}) collective-permute-start(f32[3,32,2,512]{3,1,2,0:T(8,128)S(1)} %copy.199), channel_id=1, source_target_pairs={{0,4},{4,8},{8,12},{12,16},{16,20},{20,24},{24,28},{1,5},{5,9},{9,... | collective-permute-start | bytes 1179656 | tf_op jit(solution)/shard_map/ppermute | solution.py:24
  96.5 11.9 %copy-start.26 = (s32[384]{0:T(512)S(1)}, s32[384]{0:T(512)}, u32[]{:S(2)}) copy-start(s32[384]{0:T(512)} %param.14) | copy-start | bytes 4612
  101.1 7.4 %collective-permute-start.7 = (f32[3,32,20,2]{1,2,3,0:T(8,128)}, f32[3,32,20,2]{1,2,3,0:T(8,128)}, u32[]{:S(2)}, u32[]{:S(2)}) collective-permute-start(f32[3,32,20,2]{1,2,3,0:T(8,128)} %copy.204), channel_id=1, source_target_pairs={{1,0},{2,1},{3,2},{5,4},{6,5},{7,6},{9,8},{10,9},{11,10},{13,12},{... | collective-permute-start | bytes 46088 | tf_op jit(solution)/shard_map/ppermute | solution.py:26
  104.8 6.1 %collective-permute-start.6 = (f32[3,32,20,2]{1,2,3,0:T(8,128)}, f32[3,32,20,2]{1,2,3,0:T(8,128)}, u32[]{:S(2)}, u32[]{:S(2)}) collective-permute-start(f32[3,32,20,2]{1,2,3,0:T(8,128)} %copy.203), channel_id=1, source_target_pairs={{0,1},{1,2},{2,3},{4,5},{5,6},{6,7},{8,9},{9,10},{10,11},{12,13},{... | collective-permute-start | bytes 46088 | tf_op jit(solution)/shard_map/ppermute | solution.py:24
  126.9 7.1 %copy-start.7 = (f32[3,32,16,512]{3,2,1,0:T(8,128)S(1)}, f32[3,32,16,512]{3,2,1,0:T(8,128)}, u32[]{:S(2)}) copy-start(f32[3,32,16,512]{3,2,1,0:T(8,128)} %param.12) | copy-start | bytes 9437188
  134.0 14.4 %copy-start.27 = (s32[384,1]{0,1:T(1,128)S(1)}, s32[384,1]{0,1:T(1,128)}, u32[]{:S(2)}) copy-start(s32[384,1]{0,1:T(1,128)} %param.15) | copy-start | bytes 4612
  139.9 14.4 %collective-permute-start.9 = (f32[3,32,2,512]{3,1,2,0:T(8,128)S(1)}, f32[3,32,2,512]{3,1,2,0:T(8,128)}, u32[]{:S(2)}, u32[]{:S(2)}) collective-permute-start(f32[3,32,2,512]{3,1,2,0:T(8,128)S(1)} %copy.208), channel_id=1, source_target_pairs={{4,0},{8,4},{12,8},{16,12},{20,16},{24,20},{28,24},{5,1},{9,5},{13... | collective-permute-start | bytes 1179656 | tf_op jit(solution)/shard_map/ppermute | solution.py:26
  142.0 20.9 %collective-permute-start.8 = (f32[3,32,2,512]{3,1,2,0:T(8,128)}, f32[3,32,2,512]{3,1,2,0:T(8,128)}, u32[]{:S(2)}, u32[]{:S(2)}) collective-permute-start(f32[3,32,2,512]{3,1,2,0:T(8,128)} %copy.207), channel_id=1, source_target_pairs={{0,4},{4,8},{8,12},{12,16},{16,20},{20,24},{24,28},{1,5},{5,9},{9,... | collective-permute-start | bytes 1179656 | tf_op jit(solution)/shard_map/ppermute | solution.py:24
  169.5 7.6 %collective-permute-start.11 = (f32[3,32,20,2]{1,2,3,0:T(8,128)}, f32[3,32,20,2]{1,2,3,0:T(8,128)}, u32[]{:S(2)}, u32[]{:S(2)}) collective-permute-start(f32[3,32,20,2]{1,2,3,0:T(8,128)} %copy.212), channel_id=1, source_target_pairs={{1,0},{2,1},{3,2},{5,4},{6,5},{7,6},{9,8},{10,9},{11,10},{13,12},{... | collective-permute-start | bytes 46088 | tf_op jit(solution)/shard_map/ppermute | solution.py:26
  173.2 6.3 %collective-permute-start.10 = (f32[3,32,20,2]{1,2,3,0:T(8,128)}, f32[3,32,20,2]{1,2,3,0:T(8,128)}, u32[]{:S(2)}, u32[]{:S(2)}) collective-permute-start(f32[3,32,20,2]{1,2,3,0:T(8,128)} %copy.211), channel_id=1, source_target_pairs={{0,1},{1,2},{2,3},{4,5},{5,6},{6,7},{8,9},{9,10},{10,11},{12,13},{... | collective-permute-start | bytes 46088 | tf_op jit(solution)/shard_map/ppermute | solution.py:24
  205.4 14.5 %copy-start.9 = (f32[240,1024]{1,0:T(8,128)S(1)}, f32[240,1024]{1,0:T(8,128)}, u32[]{:S(2)}) copy-start(f32[240,1024]{1,0:T(8,128)} %multiply_add_fusion.1) | copy-start | bytes 2949124
  205.4 14.5 %copy-start.21 = (f32[240,1024]{1,0:T(8,128)S(1)}, f32[240,1024]{1,0:T(8,128)}, u32[]{:S(2)}) copy-start(f32[240,1024]{1,0:T(8,128)} %param.16) | copy-start | bytes 2949124
  212.2 23.7 %copy-start.3 = (f32[3,32,16,512]{3,2,1,0:T(8,128)}, f32[3,32,16,512]{3,2,1,0:T(8,128)S(1)}, u32[]{:S(2)}) copy-start(f32[3,32,16,512]{3,2,1,0:T(8,128)S(1)} %get-tuple-element.31) | copy-start | bytes 9437188
  212.6 14.3 %collective-permute-start.13 = (f32[3,32,2,512]{3,1,2,0:T(8,128)S(1)}, f32[3,32,2,512]{3,1,2,0:T(8,128)S(1)}, u32[]{:S(2)}, u32[]{:S(2)}) collective-permute-start(f32[3,32,2,512]{3,1,2,0:T(8,128)S(1)} %copy.216), channel_id=1, source_target_pairs={{4,0},{8,4},{12,8},{16,12},{20,16},{24,20},{28,24},{5,1},{9,5},{13... | collective-permute-start | bytes 1179656 | tf_op jit(solution)/shard_map/ppermute | solution.py:26
  214.0 21.6 %collective-permute-start.12 = (f32[3,32,2,512]{3,1,2,0:T(8,128)S(1)}, f32[3,32,2,512]{3,1,2,0:T(8,128)S(1)}, u32[]{:S(2)}, u32[]{:S(2)}) collective-permute-start(f32[3,32,2,512]{3,1,2,0:T(8,128)S(1)} %copy.215), channel_id=1, source_target_pairs={{0,4},{4,8},{8,12},{12,16},{16,20},{20,24},{24,28},{1,5},{5,9},{9,... | collective-permute-start | bytes 1179656 | tf_op jit(solution)/shard_map/ppermute | solution.py:24
  240.5 7.4 %collective-permute-start.15 = (f32[3,32,20,2]{1,2,3,0:T(8,128)}, f32[3,32,20,2]{1,2,3,0:T(8,128)}, u32[]{:S(2)}, u32[]{:S(2)}) collective-permute-start(f32[3,32,20,2]{1,2,3,0:T(8,128)} %copy.220), channel_id=1, source_target_pairs={{1,0},{2,1},{3,2},{5,4},{6,5},{7,6},{9,8},{10,9},{11,10},{13,12},{... | collective-permute-start | bytes 46088 | tf_op jit(solution)/shard_map/ppermute | solution.py:26
  244.2 6.1 %collective-permute-start.14 = (f32[3,32,20,2]{1,2,3,0:T(8,128)}, f32[3,32,20,2]{1,2,3,0:T(8,128)}, u32[]{:S(2)}, u32[]{:S(2)}) collective-permute-start(f32[3,32,20,2]{1,2,3,0:T(8,128)} %copy.219), channel_id=1, source_target_pairs={{0,1},{1,2},{2,3},{4,5},{5,6},{6,7},{8,9},{9,10},{10,11},{12,13},{... | collective-permute-start | bytes 46088 | tf_op jit(solution)/shard_map/ppermute | solution.py:24
  279.1 7.0 %copy-start.30 = (s32[384]{0:T(512)S(1)}, s32[384]{0:T(512)}, u32[]{:S(2)}) copy-start(s32[384]{0:T(512)} %add_reduce_fusion) | copy-start | bytes 4612
  279.1 7.0 %copy-start.31 = (pred[384]{0:T(512)(128)(4,1)S(1)}, pred[384]{0:T(512)(128)(4,1)}, u32[]{:S(2)}) copy-start(pred[384]{0:T(512)(128)(4,1)} %compare_and_fusion) | copy-start | bytes 1156
  279.1 15.2 %copy-start.28 = (pred[1024]{0:T(1024)(128)(4,1)S(1)}, pred[1024]{0:T(1024)(128)(4,1)}, u32[]{:S(2)}) copy-start(pred[1024]{0:T(1024)(128)(4,1)} %get-tuple-element.53) | copy-start | bytes 3076
  287.5 14.2 %all-to-all-start = ((f32[3,32,32]{2,0,1:T(4,128)}), f32[3,32,32]{2,0,1:T(4,128)S(1)}, u32[]{:S(2)}, u32[]{:S(2)}) async-start(f32[3,32,32]{2,0,1:T(4,128)} %copy.224), calls=%async_computation | async-start | bytes 131072 | tf_op jit(solution)/shard_map/all_to_all | solution.py:114
  294.3 9.3 %copy-start.10 = (f32[240,1024]{1,0:T(8,128)S(1)}, f32[240,1024]{1,0:T(8,128)}, u32[]{:S(2)}) copy-start(f32[240,1024]{1,0:T(8,128)} %multiply_add_fusion.1) | copy-start | bytes 2949124
  294.3 9.2 %copy-start.20 = (f32[240,1024]{1,0:T(8,128)S(1)}, f32[240,1024]{1,0:T(8,128)}, u32[]{:S(2)}) copy-start(f32[240,1024]{1,0:T(8,128)} %add_clamp_fusion) | copy-start | bytes 2949124
  (17 other events, 49.4 us)
where the time goes:
time: 314 us; the launch traced here: 309 us
  other arithmetic  111 us (35%)
  local copies, waits for them, and re-layouts  78.1 us (25%)
  starting transfers between devices  53.9 us (17%)
  waiting for transfers between devices  48.1 us (15%)
  matrix products  16.3 us (5%)
    div x12, other arithmetic, second_diff(): (16.0 * (part(1) + part(3)) - (part(0) + part(4)) - 30.0 * part(2)) / 12.0  47.2 us
    ppermute x8, starting transfers between devices, with_halo(): lax.ppermute(tail, axis, [(i, (i + 1) % count) for i in range(ends)])  36.9 us
    ppermute x8, waiting for transfers between devices, with_halo(): lax.ppermute(tail, axis, [(i, (i + 1) % count) for i in range(ends)])  32.2 us
    concatenate x4, other arithmetic, with_halo(): jnp.concatenate([lax.ppermute(tail, axis, [(i, (i + 1) % count) for i in...  23.7 us
    add x3, other arithmetic, shards(): nxt = 2.0 * newer - older + wave_accel(depth_pad(padded), speeds)  16.4 us
    dot_general x4, matrix products, shards(): jnp.dot(stiffness[kind], disp_next, precision=lax.Precision.HIGHEST)  15.4 us
    ppermute x8, waiting for transfers between devices, with_halo(): lax.ppermute(head, axis, [((i + 1) % count, i) for i in range(ends)])  14.5 us
    slice x11, local copies, waits for them, and re-layouts, with_halo(): lax.slice_in_dim(cells, cells.shape[dim] - width, cells.shape[dim], axis=...  14.2 us
  transfers between devices with their start and end apart: 17, of which 9 were waited for; matrix products, arithmetic and copies ran while one was open for 15% of the time, Pallas kernels for 0%

commit v1 on v0

v1 whole, which is shorter than its diff:
```python
import functools

import jax
import jax.numpy as jnp
from jax import lax
from jax.experimental import pallas as pl
from jax.experimental.pallas import tpu as pltpu
from jax.sharding import PartitionSpec as P

STEPS = 4
time_step = 0.5
damping = 0.1
yield_drift = 0.5
hyst_stiff = 1.0
ground_gain = 0.1
LANES = 128
HIGHEST = lax.Precision.HIGHEST
MESH = pl.DeviceIdType.MESH


def wave_kernel(
    n_gx, n_gy, capacity,
    u_prev, u_now, speeds, site_row, site_col, route_row, route_col,
    frame_disp, frame_vel, frame_acc, frame_hyst, kind_row, stiffness,
    before_out, last_out, disp_out, hyst_out, part_acc, part_vel, outgoing,
    lev_a, lev_b, spd, xsend, xrecv, ysend, yrecv,
    fd, fv, fa, fh, stiff, f_acc, f_vel, pick, placing, third, ground,
    load_sem, store_sem, xs_sem, xr_sem, ys_sem, yr_sem,
):
    ncomp, nz, cx, cy = u_now.shape
    gx = lax.axis_index("gx")
    gy = lax.axis_index("gy")
    has = (gx > 0, gx < n_gx - 1, gy > 0, gy < n_gy - 1)
    peer = ({"gx": gx - 1}, {"gx": gx + 1}, {"gy": gy - 1}, {"gy": gy + 1})

    loads = []

    def load(src, dst):
        copy = pltpu.make_async_copy(src, dst, load_sem.at[len(loads)])
        copy.start()
        loads.append(copy)
        return copy

    now_in = [load(u_now.at[c], lev_b.at[c, pl.ds(2, nz)]) for c in range(ncomp)]
    frames_in = [
        load(frame_disp, fd), load(frame_vel, fv), load(frame_acc, fa),
        load(frame_hyst, fh), load(stiffness, stiff),
    ]
    spd_in = load(speeds, spd)
    prev_in = [load(u_prev.at[c], lev_a.at[c, pl.ds(2, nz)]) for c in range(ncomp)]

    barrier = pltpu.get_barrier_semaphore()
    for d in range(4):
        @pl.when(has[d])
        def _(d=d):
            pl.semaphore_signal(barrier, inc=1, device_id=peer[d], device_id_type=MESH)

    rim = jnp.zeros((2, cx, cy), jnp.float32)
    for lev in (lev_a, lev_b):
        for c in range(ncomp):
            lev[c, pl.ds(0, 2)] = rim
            lev[c, pl.ds(nz + 2, 2)] = rim

    for side in range(2):
        @pl.when(jnp.logical_not(has[side]))
        def _(side=side):
            empty = jnp.zeros((2, nz, cy), jnp.float32)
            for k in range(STEPS):
                for c in range(ncomp):
                    xrecv[k, c, side] = empty

        @pl.when(jnp.logical_not(has[2 + side]))
        def _(side=side):
            for k in range(STEPS):
                for c in range(ncomp):
                    yrecv[k, c, side] = jnp.zeros((cx, LANES), jnp.float32)

    pl.semaphore_wait(barrier, sum(h.astype(jnp.int32) for h in has))

    def halo_copy(k, c, d):
        if d < 2:
            send, recv, ss, rs = xsend, xrecv, xs_sem, xr_sem
        else:
            send, recv, ss, rs = ysend, yrecv, ys_sem, yr_sem
        mine = d % 2
        return pltpu.make_async_remote_copy(
            src_ref=send.at[k, c, mine],
            dst_ref=recv.at[k, c, 1 - mine],
            send_sem=ss.at[k, c, mine],
            recv_sem=rs.at[k, c, 1 - mine],
            device_id=peer[d],
            device_id_type=MESH,
        )

    def send_halo(k, c):
        for d in range(4):
            @pl.when(has[d])
            def _(d=d):
                halo_copy(k, c, d).start()

    def wait_halo(k, c):
        for d in range(4):
            @pl.when(has[d])
            def _(d=d):
                recv, ss, rs = (xrecv, xs_sem, xr_sem) if d < 2 else (yrecv, ys_sem, yr_sem)
                pltpu.make_async_remote_copy(
                    src_ref=recv.at[k, c, d % 2],
                    dst_ref=recv.at[k, c, d % 2],
                    send_sem=ss.at[k, c, d % 2],
                    recv_sem=rs.at[k, c, d % 2],
                    device_id=peer[d],
                    device_id_type=MESH,
                ).wait_recv()

    def wait_sent(k, c):
        for d in range(4):
            @pl.when(has[d])
            def _(d=d):
                halo_copy(k, c, d).wait_send()

    lane = lax.broadcasted_iota(jnp.int32, (cx, LANES), 1)
    lane_plane = lane >> 1
    row = lax.broadcasted_iota(jnp.int32, (cx, cy), 0)

    def pack_edges(k, c, z, v, acc):
        head, tail = acc
        xsend[k, c, 0, 0, pl.ds(z, 1), :] = v[0:1]
        xsend[k, c, 0, 1, pl.ds(z, 1), :] = v[1:2]
        xsend[k, c, 1, 0, pl.ds(z, 1), :] = v[cx - 2:cx - 1]
        xsend[k, c, 1, 1, pl.ds(z, 1), :] = v[cx - 1:cx]
        here = lane_plane == z
        head = jnp.where(here, pltpu.roll(v[:, :LANES], 2 * z, 1), head)
        tail = jnp.where(here, pltpu.roll(v[:, cy - LANES:], 2 * z + 2, 1), tail)
        return head, tail

    blank = (jnp.zeros((cx, LANES), jnp.float32),) * 2

    def put_y(k, c, acc):
        ysend[k, c, 0] = acc[0]
        ysend[k, c, 1] = acc[1]

    def wave_step(k, c, older, newer):
        def plane(z, acc):
            u = newer[c, z + 2]
            deep = 16.0 * (newer[c, z + 1] + newer[c, z + 3]) - (newer[c, z] + newer[c, z + 4])
            xl0 = xrecv[k, c, 0, 0, pl.ds(z, 1), :]
            xl1 = xrecv[k, c, 0, 1, pl.ds(z, 1), :]
            xr0 = xrecv[k, c, 1, 0, pl.ds(z, 1), :]
            xr1 = xrecv[k, c, 1, 1, pl.ds(z, 1), :]
            w1 = jnp.where(row == 0, xl1, pltpu.roll(u, 1, 0))
            w2 = jnp.where(row == 0, xl0, jnp.where(row == 1, xl1, pltpu.roll(u, 2, 0)))
            e1 = jnp.where(row == cx - 1, xr0, pltpu.roll(u, cx - 1, 0))
            e2 = jnp.where(row == cx - 2, xr0, jnp.where(row == cx - 1, xr1, pltpu.roll(u, cx - 2, 0)))
            east = 16.0 * (w1 + e1) - (w2 + e2)
            yl = yrecv[k, c, 0]
            yr = yrecv[k, c, 1]

            def first(values, count, fix):
                return jnp.concatenate(
                    [jnp.where(lane < count, fix, values[:, :LANES]), values[:, LANES:]], axis=1
                )

            def final(values, count, fix):
                return jnp.concatenate(
                    [
                        values[:, :cy - LANES],
                        jnp.where(lane >= LANES - count, fix, values[:, cy - LANES:]),
                    ],
                    axis=1,
                )

            back = LANES - 1 - 2 * z
            s1 = first(pltpu.roll(u, 1, 1), 1, pltpu.roll(yl, back, 1))
            s2 = first(pltpu.roll(u, 2, 1), 2, pltpu.roll(yl, lax.rem(back + 1, LANES), 1))
            n1 = final(pltpu.roll(u, cy - 1, 1), 1, pltpu.roll(yr, back, 1))
            n2 = final(pltpu.roll(u, cy - 2, 1), 2, pltpu.roll(yr, back - 1, 1))
            north = 16.0 * (s1 + n1) - (s2 + n2)
            parts = [east, north, deep]
            own = parts.pop(c)
            accel = spd[0, z] * (own - 30.0 * u) + spd[1, z] * (parts[0] + parts[1] - 60.0 * u)
            v = 2.0 * u - older[c, z + 2] + accel * (1.0 / 12.0)
            older[c, z + 2] = v
            if k < STEPS - 1:
                return pack_edges(k + 1, c, z, v, acc)
            return acc

        acc = lax.fori_loop(0, nz, plane, blank)
        if k < STEPS - 1:
            put_y(k + 1, c, acc)

    for c in range(ncomp):
        now_in[c].wait()
        acc = lax.fori_loop(
            0, nz, lambda z, acc, c=c: pack_edges(0, c, z, lev_b[c, z + 2], acc), blank
        )
        put_y(0, c, acc)
        send_halo(0, c)

    for copy in frames_in:
        copy.wait()
    nf, slots = fd.shape
    wide = 2 * LANES

    def frames(i, carry):
        cols = pl.ds(pl.multiple_of(i * wide, wide), wide)
        frow = lax.broadcasted_iota(jnp.int32, (nf, wide), 0)
        d0, v0, a0 = fd[:, cols], fv[:, cols], fa[:, cols]
        change = time_step * v0 + 0.5 * time_step * time_step * a0
        nxt = d0 + change
        moved = nxt - d0
        drift = moved - jnp.where(frow < 3, 0.0, pltpu.roll(moved, 3, 0))
        hyst = jnp.clip(fh[:, cols] + drift, -yield_drift, yield_drift)
        fd[:, cols] = nxt
        fh[:, cols] = hyst
        kinds = kind_row[:, cols]
        total = (-damping) * (v0 + 0.5 * time_step * a0) - hyst_stiff * (
            hyst - jnp.where(frow >= nf - 3, 0.0, pltpu.roll(hyst, nf - 3, 0))
        )
        for kind in range(stiff.shape[0]):
            product = jnp.dot(
                stiff[kind], nxt, precision=HIGHEST, preferred_element_type=jnp.float32
            )
            total = total - jnp.where(kinds == kind, product, 0.0)
        f_acc[:, cols] = total
        f_vel[:, cols] = v0 + 0.5 * time_step * (a0 + total)
        return carry

    lax.fori_loop(0, slots // wide, frames, 0)
    stores = []

    def store(src, dst):
        copy = pltpu.make_async_copy(src, dst, store_sem.at[len(stores)])
        copy.start()
        stores.append(copy)

    store(fd, disp_out)
    store(fh, hyst_out)
    store(f_acc, part_acc)
    store(f_vel, part_vel)

    count = route_row.shape[1]
    pick[...] = (
        lax.broadcasted_iota(jnp.int32, (cy, count), 0) == site_col[...]
    ).astype(jnp.float32)
    routes = route_col[...]
    ids_i = lax.broadcasted_iota(jnp.int32, (count, count), 0)
    ids_j = lax.broadcasted_iota(jnp.int32, (count, count), 1)
    same = jnp.logical_and(routes == route_row[...], ids_j < ids_i)
    rank = jnp.sum(same.astype(jnp.float32), axis=1, keepdims=True).astype(jnp.int32)
    slot = routes * capacity + rank
    placing[...] = (
        lax.broadcasted_iota(jnp.int32, (count, slots), 1) == slot
    ).astype(jnp.float32)

    spd_in.wait()
    for copy in prev_in:
        copy.wait()

    for k in range(STEPS):
        older, newer = (lev_a, lev_b) if k % 2 == 0 else (lev_b, lev_a)
        for c in range(ncomp):
            wait_halo(k, c)
            if k == STEPS - 1:
                third[c] = older[c, 2]
            wave_step(k, c, older, newer)
            if k < STEPS - 1:
                send_halo(k + 1, c)
            if k == STEPS - 2:
                store(older.at[c, pl.ds(2, nz)], before_out.at[c])
            if k == STEPS - 1:
                store(older.at[c, pl.ds(2, nz)], last_out.at[c])
                ground[c] = ground_gain * (older[c, 2] - 2.0 * newer[c, 2] + third[c])

    cells = jnp.dot(
        ground[...].reshape(ncomp * cx, cy), pick[...],
        precision=HIGHEST, preferred_element_type=jnp.float32,
    )
    at_row = lax.broadcasted_iota(jnp.int32, (cx, count), 0) == site_row[...]
    motion = [
        jnp.sum(jnp.where(at_row, cells[c * cx:(c + 1) * cx], 0.0), axis=0, keepdims=True)
        for c in range(ncomp)
    ]
    motion = jnp.concatenate(
        motion + [jnp.zeros((8 - ncomp, count), jnp.float32)], axis=0
    )
    outgoing[...] = jnp.dot(
        motion, placing[...], precision=HIGHEST, preferred_element_type=jnp.float32
    )
    for k in range(STEPS):
        for c in range(ncomp):
            wait_sent(k, c)
    for copy in stores:
        copy.wait()


def forcing_kernel(moved_ref, acc_ref, vel_ref, acc_out, vel_out):
    nf, width = acc_ref.shape
    ids = lax.broadcasted_iota(jnp.int32, (nf, width), 0)
    phase = ids - 3 * ((ids * 43691) >> 17)
    force = jnp.where(
        phase == 0, moved_ref[0:1], jnp.where(phase == 1, moved_ref[1:2], moved_ref[2:3])
    )
    acc_out[...] = acc_ref[...] - force
    vel_out[...] = vel_ref[...] - (0.5 * time_step) * force


def shards(
    n_gx, n_gy,
    u_prev, u_now, speeds, sites, routes,
    frame_disp, frame_vel, frame_acc, frame_hyst, frame_kind, stiffness,
):
    ncomp, nz, cx, cy = u_now.shape
    devices = n_gx * n_gy
    nf, slots = frame_disp.shape
    capacity = slots // devices
    count = sites.shape[0]
    f32 = jnp.float32
    site_row = (sites // cy).reshape(1, count)
    site_col = (sites % cy).reshape(1, count)
    field = jax.ShapeDtypeStruct(u_now.shape, f32)
    frame = jax.ShapeDtypeStruct(frame_disp.shape, f32)
    anyspec = pl.BlockSpec(memory_space=pl.ANY)
    vmem = pl.BlockSpec(memory_space=pltpu.VMEM)
    level = pltpu.VMEM((ncomp, nz + 4, cx, cy), f32)
    before, last, disp, hyst, part_acc, part_vel, outgoing = pl.pallas_call(
        functools.partial(wave_kernel, n_gx, n_gy, capacity),
        out_shape=(field, field, frame, frame, frame, frame,
                   jax.ShapeDtypeStruct((8, slots), f32)),
        in_specs=[anyspec] * 3 + [vmem] * 4 + [anyspec] * 4 + [vmem, anyspec],
        out_specs=(anyspec,) * 6 + (vmem,),
        scratch_shapes=[
            level, level,
            pltpu.VMEM(speeds.shape, f32),
            pltpu.VMEM((STEPS, ncomp, 2, 2, nz, cy), f32),
            pltpu.VMEM((STEPS, ncomp, 2, 2, nz, cy), f32),
            pltpu.VMEM((STEPS, ncomp, 2, cx, LANES), f32),
            pltpu.VMEM((STEPS, ncomp, 2, cx, LANES), f32),
            pltpu.VMEM((nf, slots), f32), pltpu.VMEM((nf, slots), f32),
            pltpu.VMEM((nf, slots), f32), pltpu.VMEM((nf, slots), f32),
            pltpu.VMEM(stiffness.shape, f32),
            pltpu.VMEM((nf, slots), f32), pltpu.VMEM((nf, slots), f32),
            pltpu.VMEM((cy, count), f32),
            pltpu.VMEM((count, slots), f32),
            pltpu.VMEM((ncomp, cx, cy), f32),
            pltpu.VMEM((ncomp, cx, cy), f32),
            pltpu.SemaphoreType.DMA((2 * ncomp + 6,)),
            pltpu.SemaphoreType.DMA((2 * ncomp + 4,)),
            pltpu.SemaphoreType.DMA((STEPS, ncomp, 2)),
            pltpu.SemaphoreType.DMA((STEPS, ncomp, 2)),
            pltpu.SemaphoreType.DMA((STEPS, ncomp, 2)),
            pltpu.SemaphoreType.DMA((STEPS, ncomp, 2)),
        ],
        compiler_params=pltpu.CompilerParams(
            collective_id=0, has_side_effects=True, vmem_limit_bytes=52 * 1024 * 1024
        ),
        name="wave",
    )(
        u_prev, u_now, speeds, site_row, site_col, routes.reshape(1, count), routes,
        frame_disp, frame_vel, frame_acc, frame_hyst, frame_kind.reshape(1, slots), stiffness,
    )
    parcels = outgoing[:ncomp].reshape(ncomp, devices, capacity)
    arrived = lax.all_to_all(parcels, ("gx", "gy"), split_axis=1, concat_axis=1, tiled=True)
    moved = arrived.reshape(ncomp, slots)
    wide = min(slots, 4 * LANES)
    block = pl.BlockSpec((nf, wide), lambda i: (0, i))
    acc_next, vel_next = pl.pallas_call(
        forcing_kernel,
        grid=(slots // wide,),
        out_shape=(frame, frame),
        in_specs=[pl.BlockSpec((ncomp, wide), lambda i: (0, i)), block, block],
        out_specs=(block, block),
        name="forcing",
    )(moved, part_acc, part_vel)
    return before, last, disp, vel_next, acc_next, hyst


def solution(mesh):
    cells = P(None, None, "gx", "gy")
    both = ("gx", "gy")
    frame = P(None, both)
    return jax.shard_map(
        functools.partial(shards, mesh.shape["gx"], mesh.shape["gy"]),
        mesh=mesh,
        in_specs=(cells, cells, cells, P(both), P(both, None), frame, frame, frame, frame,
                  P(both), P()),
        out_specs=(cells, cells, frame, frame, frame, frame),
        check_vma=False,
    )
```

time: 314 us -> 113 us (0.36); the launches traced: 309 us -> 112 us
  other arithmetic: 111 us -> 0.69 us
  Pallas kernels: 0 us -> 83.9 us
  local copies, waits for them, and re-layouts: 78.1 us -> 11.5 us
  starting transfers between devices: 53.9 us -> 8.19 us
  waiting for transfers between devices: 48.1 us -> 7.41 us
  matrix products: 16.3 us -> 0 us
    pallas_call x0 -> x2, Pallas kernels: none -> 83.9 us  [the longest x1 81.3 us: shards(): pl.pallas_call(functools.partial(wave_kernel, n_gx, n_gy, capacity), out_...]
    div x12 -> x0, other arithmetic: 47.2 us -> none  [second_diff(): (16.0 * (part(1) + part(3)) - (part(0) + part(4)) - 30.0 * part(2)) / 12.0]
    ppermute x16 -> x0, starting transfers between devices: 47.2 us -> none  [the longest x8 36.9 us: with_halo(): lax.ppermute(tail, axis, [(i, (i + 1) % count) for i in range(ends)])]
    ppermute x16 -> x0, waiting for transfers between devices: 46.7 us -> none  [the longest x8 32.2 us: with_halo(): lax.ppermute(tail, axis, [(i, (i + 1) % count) for i in range(ends)])]
    slice x31 -> x1, local copies, waits for them, and re-layouts: 39.1 us -> 0.01 us  [shards(): parcels = outgoing[:ncomp].reshape(ncomp, devices, capacity)]
    ppermute x16 -> x0, local copies, waits for them, and re-layouts: 23.7 us -> none  [the longest x8 12 us: with_halo(): lax.ppermute(tail, axis, [(i, (i + 1) % count) for i in range(ends)])]
    concatenate x4 -> x0, other arithmetic: 23.7 us -> none  [with_halo(): jnp.concatenate([lax.ppermute(tail, axis, [(i, (i + 1) % count) for i in...]
    add x5 -> x0, other arithmetic: 20.1 us -> none  [the longest x3 16.4 us: shards(): nxt = 2.0 * newer - older + wave_accel(depth_pad(padded), speeds)]
  transfers between devices with their start and end apart: 17 -> 1, of which waited for: 9 -> 1; matrix products, arithmetic and copies ran while one was open for 15% -> 0% of each run, Pallas kernels for 0% -> 0%
where the time goes in v1:
time: 113 us; the launch traced here: 112 us
  Pallas kernels  83.9 us (74%)
  local copies, waits for them, and re-layouts  11.5 us (10%)
  starting transfers between devices  8.19 us (7%)
  waiting for transfers between devices  7.41 us (7%)
    pallas_call x1, Pallas kernels, shards(): pl.pallas_call(functools.partial(wave_kernel, n_gx, n_gy, capacity), out_...  81.3 us
    unnamed x13, local copies, waits for them, and re-layouts  10 us
    all_to_all x1, starting transfers between devices, shards(): lax.all_to_all(parcels, ('gx', 'gy'), split_axis=1, concat_axis=1, tiled=...  8.19 us
    all_to_all x1, waiting for transfers between devices, shards(): lax.all_to_all(parcels, ('gx', 'gy'), split_axis=1, concat_axis=1, tiled=...  7.41 us
    pallas_call x1, Pallas kernels, shards(): pl.pallas_call(forcing_kernel, grid=(slots // wide,), out_shape=(frame, f...  2.55 us
  transfers between devices with their start and end apart: 1, of which 1 were waited for; matrix products, arithmetic and copies ran while one was open for 0% of the time, Pallas kernels for 0%

profile of v1, /device:TPU:0, one launch (start us, length us, event | category | flops | bytes accessed | tf_op | source)
XLA Modules:
  0.0 112.3 jit_solution(16109723003712444580)
XLA Ops:
  0.6 0.7 add_select_fusion
  1.3 0.8 copy.18.route_col
  2.2 0.0 copy-start
  2.2 0.7 copy-done
  2.8 0.0 copy-start.1
  2.8 0.7 copy-done.1
  3.5 81.3 %wave.1 = (f32[3,32,16,512]{3,2,1,0:T(8,128)}, f32[3,32,16,512]{3,2,1,0:T(8,128)}, f32[240,1024]{1,0:T(8,128)S(1)}, f32[240,1024]{1,0:T(8,128)}, f32[240,1024]{1...) custom-call(f32[3,32,16,512]{3,2,1,0:T(8,128)} %u_prev.1, f32[3,32,16,512]{3,2,1,0:T(8,128)} %u_now.1, ...), custom_call_target="tpu_custom_call" | custom-call | tf_op jit(solution)/shard_map/wave/pallas_call | solution.py:325
  84.9 0.1 reshape.34
  85.0 0.7 copy.19
  85.6 8.2 %all-to-all-start = ((f32[3,32,32]{2,0,1:T(4,128)}), f32[3,32,32]{2,0,1:T(4,128)S(1)}, u32[]{:S(2)}, u32[]{:S(2)}) async-start(f32[3,32,32]{2,0,1:T(4,128)} %copy.19), calls=%async_computation | async-start | bytes 131072 | tf_op jit(solution)/shard_map/all_to_all | solution.py:362
  93.8 7.4 %all-to-all-done = f32[3,32,32]{2,0,1:T(4,128)S(1)} async-done(((f32[3,32,32]{2,0,1:T(4,128)}), f32[3,32,32]{2,0,1:T(4,128)S(1)}, u32[]{:S(2)}, u32[]{:S(2)}) %all-to-all-start) | async-done | bytes 12320 | tf_op jit(solution)/shard_map/all_to_all | solution.py:362
  101.2 0.7 reshape.35.moved_ref
  101.9 2.6 %forcing.1 = (f32[240,1024]{1,0:T(8,128)}, f32[240,1024]{1,0:T(8,128)}) custom-call(f32[3,1024]{1,0:T(4,128)} %reshape.35.moved_ref, f32[240,1024]{1,0:T(8,128)} %get-tuple-element.19.acc_ref, f32[240,1024]{1,0:T(8,128)} %get-tuple-element.20.vel_ref), custom_call_target="tpu_custom_call" | custom-call | tf_op jit(solution)/shard_map/forcing/pallas_call | solution.py:366
  104.5 0.0 copy-start.2
  104.5 4.3 %copy.25 = f32[3,32,16,512]{3,2,1,0:T(8,128)} copy(f32[3,32,16,512]{3,2,1,0:T(8,128)} %get-tuple-element.32) | data formatting | bytes 6291456
  108.8 0.0 copy-done.2
  108.8 0.0 copy-start.3
  108.8 1.7 %copy.26 = f32[3,32,16,512]{3,2,1,0:T(8,128)} copy(f32[3,32,16,512]{3,2,1,0:T(8,128)S(1)} %copy-done.2) | data formatting | bytes 6291456
  110.4 0.9 copy.27
  111.4 0.0 copy-done.3
  111.4 0.9 copy.28
  (4 shorter events, 0.0 us)
Async XLA Ops:
  2.2 0.7 copy-start
  2.8 0.7 copy-start.1
  85.6 15.6 %all-to-all-start = ((f32[3,32,32]{2,0,1:T(4,128)}), f32[3,32,32]{2,0,1:T(4,128)S(1)}, u32[]{:S(2)}, u32[]{:S(2)}) async-start(f32[3,32,32]{2,0,1:T(4,128)} %copy.19), calls=%async_computation | async-start | bytes 131072 | tf_op jit(solution)/shard_map/all_to_all | solution.py:362
  104.5 4.3 %copy-start.2 = (f32[3,32,16,512]{3,2,1,0:T(8,128)S(1)}, f32[3,32,16,512]{3,2,1,0:T(8,128)}, u32[]{:S(2)}) copy-start(f32[3,32,16,512]{3,2,1,0:T(8,128)} %get-tuple-element.33) | copy-start | bytes 9437188
  108.8 2.6 %copy-start.3 = (f32[240,1024]{1,0:T(8,128)S(1)}, f32[240,1024]{1,0:T(8,128)}, u32[]{:S(2)}) copy-start(f32[240,1024]{1,0:T(8,128)} %get-tuple-element.37) | copy-start | bytes 2949124

commit v2 on v1

v2 whole, which is shorter than its diff:
```python
import functools

import jax
import jax.numpy as jnp
from jax import lax
from jax.experimental import pallas as pl
from jax.experimental.pallas import tpu as pltpu
from jax.sharding import PartitionSpec as P

STEPS = 4
time_step = 0.5
damping = 0.1
yield_drift = 0.5
hyst_stiff = 1.0
ground_gain = 0.1
LANES = 128
HIGHEST = lax.Precision.HIGHEST
MESH = pl.DeviceIdType.MESH


def lines(n_gx, n_gy):
    return (("gy", n_gy), ("gx", n_gx))


def wave_kernel(
    n_gx, n_gy, capacity,
    u_prev, u_now, speeds, sites, routes,
    frame_disp, frame_vel, frame_acc, frame_hyst, frame_kind, stiffness,
    before_out, last_out, disp_out, vel_out, acc_out, hyst_out,
    lev_a, lev_b, spd, xsend, xrecv, ysend, yrecv,
    fd, fv, fa, fh, stiff, f_acc, f_vel, site_row, route_row, kind_row,
    pick, placing, third, ground, send_1, recv_1, send_2, recv_2, moved,
    load_sem, store_sem, xs_sem, xr_sem, ys_sem, yr_sem,
    send_1_sem, recv_1_sem, send_2_sem, recv_2_sem,
):
    ncomp, nz, cx, cy = u_now.shape
    tiles = cy // LANES
    place = {"gx": lax.axis_index("gx"), "gy": lax.axis_index("gy")}
    gx, gy = place["gx"], place["gy"]
    has = (gx > 0, gx < n_gx - 1, gy > 0, gy < n_gy - 1)
    peer = ({"gx": gx - 1}, {"gx": gx + 1}, {"gy": gy - 1}, {"gy": gy + 1})

    loads = []

    def load(src, dst):
        copy = pltpu.make_async_copy(src, dst, load_sem.at[len(loads)])
        copy.start()
        loads.append(copy)
        return copy

    now_in = [load(u_now.at[c], lev_b.at[c, pl.ds(2, nz)]) for c in range(ncomp)]
    field_in = [load(speeds, spd)] + [
        load(u_prev.at[c], lev_a.at[c, pl.ds(2, nz)]) for c in range(ncomp)
    ]
    frames_in = [
        load(frame_disp, fd), load(frame_vel, fv), load(frame_acc, fa),
        load(frame_hyst, fh), load(stiffness, stiff),
        load(frame_kind, kind_row), load(sites, site_row), load(routes, route_row),
    ]

    barrier = pltpu.get_barrier_semaphore()
    for axis, size in lines(n_gx, n_gy):
        for off in range(1, size):
            pl.semaphore_signal(
                barrier, inc=1, device_id={axis: lax.rem(place[axis] + off, size)},
                device_id_type=MESH,
            )

    rim = jnp.zeros((2, cx, cy), jnp.float32)
    for lev in (lev_a, lev_b):
        for c in range(ncomp):
            lev[c, pl.ds(0, 2)] = rim
            lev[c, pl.ds(nz + 2, 2)] = rim

    for side in range(2):
        @pl.when(jnp.logical_not(has[side]))
        def _(side=side):
            empty = jnp.zeros(xrecv.shape[3:], jnp.float32)
            for k in range(STEPS):
                for c in range(ncomp):
                    xrecv[k, c, side] = empty

        @pl.when(jnp.logical_not(has[2 + side]))
        def _(side=side):
            for k in range(STEPS):
                for c in range(ncomp):
                    for t in range(2):
                        yrecv[k, c, t, side] = jnp.zeros((cx, LANES), jnp.float32)

    pl.semaphore_wait(barrier, n_gx + n_gy - 2)

    def planes(k, t):
        cut = 2 * (STEPS - k) - 1
        return (0, cut) if t == 0 else (cut, nz)

    def halo_copy(k, c, t, d):
        mine = d % 2
        if d < 2:
            low, high = planes(k, t)
            zs = pl.ds(low, high - low)
            src, dst = xsend.at[k, c, mine, zs], xrecv.at[k, c, 1 - mine, zs]
            ss, rs = xs_sem, xr_sem
        else:
            src, dst = ysend.at[k, c, t, mine], yrecv.at[k, c, t, 1 - mine]
            ss, rs = ys_sem, yr_sem
        return pltpu.make_async_remote_copy(
            src_ref=src, dst_ref=dst,
            send_sem=ss.at[k, c, t, mine], recv_sem=rs.at[k, c, t, 1 - mine],
            device_id=peer[d], device_id_type=MESH,
        )

    def send_halo(k, c, t):
        for d in range(4):
            @pl.when(has[d])
            def _(d=d):
                halo_copy(k, c, t, d).start()

    def wait_halo(k, c, t):
        low, high = planes(k, t)
        zs = pl.ds(low, high - low)
        for d in range(4):
            @pl.when(has[d])
            def _(d=d):
                if d < 2:
                    slot, ss, rs = xrecv.at[k, c, d % 2, zs], xs_sem, xr_sem
                else:
                    slot, ss, rs = yrecv.at[k, c, t, d % 2], ys_sem, yr_sem
                pltpu.make_async_remote_copy(
                    src_ref=slot, dst_ref=slot,
                    send_sem=ss.at[k, c, t, d % 2], recv_sem=rs.at[k, c, t, d % 2],
                    device_id=peer[d], device_id_type=MESH,
                ).wait_recv()

    def wait_sent(k, c, t):
        for d in range(4):
            @pl.when(has[d])
            def _(d=d):
                halo_copy(k, c, t, d).wait_send()

    lane = lax.broadcasted_iota(jnp.int32, (cx, LANES), 1)
    lane_plane = lane >> 1
    row = lax.broadcasted_iota(jnp.int32, (cx, cy), 0)

    def pack_edges(k, c, z, v, acc):
        head, tail = acc
        for side in range(2):
            for r in range(2):
                at = r if side == 0 else cx - 2 + r
                for t in range(tiles):
                    xsend[k, c, side, z, pl.ds(r * tiles + t, 1), :] = (
                        v[at:at + 1, t * LANES:(t + 1) * LANES]
                    )
        here = lane_plane == z
        head = jnp.where(here, pltpu.roll(v[:, :LANES], 2 * z, 1), head)
        tail = jnp.where(here, pltpu.roll(v[:, cy - LANES:], lax.rem(2 * z + 2, LANES), 1), tail)
        return head, tail

    blank = (jnp.zeros((cx, LANES), jnp.float32),) * 2

    def put_y(k, c, t, acc):
        ysend[k, c, t, 0] = acc[0]
        ysend[k, c, t, 1] = acc[1]

    def wave_part(k, c, low, high, t, older, newer, acc):
        def plane(z, acc):
            u = newer[c, z + 2]
            deep = 16.0 * (newer[c, z + 1] + newer[c, z + 3]) - (newer[c, z] + newer[c, z + 4])

            def edge(side, r):
                return jnp.concatenate(
                    [xrecv[k, c, side, z, pl.ds(r * tiles + i, 1), :] for i in range(tiles)],
                    axis=1,
                )

            xl0, xl1, xr0, xr1 = edge(0, 0), edge(0, 1), edge(1, 0), edge(1, 1)
            w1 = jnp.where(row == 0, xl1, pltpu.roll(u, 1, 0))
            w2 = jnp.where(row == 0, xl0, jnp.where(row == 1, xl1, pltpu.roll(u, 2, 0)))
            e1 = jnp.where(row == cx - 1, xr0, pltpu.roll(u, cx - 1, 0))
            e2 = jnp.where(row == cx - 2, xr0, jnp.where(row == cx - 1, xr1, pltpu.roll(u, cx - 2, 0)))
            east = 16.0 * (w1 + e1) - (w2 + e2)
            yl = yrecv[k, c, t, 0]
            yr = yrecv[k, c, t, 1]

            def first(values, count, fix):
                return jnp.concatenate(
                    [jnp.where(lane < count, fix, values[:, :LANES]), values[:, LANES:]], axis=1
                )

            def final(values, count, fix):
                return jnp.concatenate(
                    [
                        values[:, :cy - LANES],
                        jnp.where(lane >= LANES - count, fix, values[:, cy - LANES:]),
                    ],
                    axis=1,
                )

            back = LANES - 1 - 2 * z
            s1 = first(pltpu.roll(u, 1, 1), 1, pltpu.roll(yl, back, 1))
            s2 = first(pltpu.roll(u, 2, 1), 2, pltpu.roll(yl, lax.rem(back + 1, LANES), 1))
            n1 = final(pltpu.roll(u, cy - 1, 1), 1, pltpu.roll(yr, back, 1))
            n2 = final(pltpu.roll(u, cy - 2, 1), 2, pltpu.roll(yr, back - 1, 1))
            north = 16.0 * (s1 + n1) - (s2 + n2)
            parts = [east, north, deep]
            own = parts.pop(c)
            accel = spd[0, z] * (own - 30.0 * u) + spd[1, z] * (parts[0] + parts[1] - 60.0 * u)
            v = 2.0 * u - older[c, z + 2] + accel * (1.0 / 12.0)
            older[c, z + 2] = v
            if k < STEPS - 1:
                return pack_edges(k + 1, c, z, v, acc)
            return acc

        return lax.fori_loop(low, high, plane, acc)

    def levels(k):
        return (lev_a, lev_b) if k % 2 == 0 else (lev_b, lev_a)

    def top_step(k):
        older, newer = levels(k)
        low, high = planes(k, 0)
        for c in range(ncomp):
            wait_halo(k, c, 0)
            if k == STEPS - 1:
                third[c] = older[c, 2]
                wave_part(k, c, low, high, 0, older, newer, blank)
                ground[c] = ground_gain * (older[c, 2] - 2.0 * newer[c, 2] + third[c])
            else:
                cut = planes(k + 1, 0)[1]
                acc = wave_part(k, c, low, cut, 0, older, newer, blank)
                put_y(k + 1, c, 0, acc)
                send_halo(k + 1, c, 0)
                acc = wave_part(k, c, cut, high, 0, older, newer, blank)
                put_y(k + 1, c, 1, acc)

    def deep_step(k, c):
        older, newer = levels(k)
        low, high = planes(k, 1)
        wait_halo(k, c, 1)
        if k < STEPS - 1:
            acc = (ysend[k + 1, c, 1, 0], ysend[k + 1, c, 1, 1])
            acc = wave_part(k, c, low, high, 1, older, newer, acc)
            put_y(k + 1, c, 1, acc)
            send_halo(k + 1, c, 1)
        else:
            wave_part(k, c, low, high, 1, older, newer, blank)

    def first_edges(c, t):
        low, high = planes(0, t)
        acc = lax.fori_loop(
            low, high, lambda z, acc: pack_edges(0, c, z, lev_b[c, z + 2], acc), blank
        )
        put_y(0, c, t, acc)
        send_halo(0, c, t)

    stores = []

    def store(src, dst):
        copy = pltpu.make_async_copy(src, dst, store_sem.at[len(stores)])
        copy.start()
        stores.append(copy)

    nf, slots = fd.shape
    wide = 2 * LANES

    def frames(i, carry):
        cols = pl.ds(pl.multiple_of(i * wide, wide), wide)
        frow = lax.broadcasted_iota(jnp.int32, (nf, wide), 0)
        d0, v0, a0 = fd[:, cols], fv[:, cols], fa[:, cols]
        change = time_step * v0 + 0.5 * time_step * time_step * a0
        nxt = d0 + change
        moving = nxt - d0
        drift = moving - jnp.where(frow < 3, 0.0, pltpu.roll(moving, 3, 0))
        hyst = jnp.clip(fh[:, cols] + drift, -yield_drift, yield_drift)
        fd[:, cols] = nxt
        fh[:, cols] = hyst
        kinds = kind_row[:, cols]
        total = (-damping) * (v0 + 0.5 * time_step * a0) - hyst_stiff * (
            hyst - jnp.where(frow >= nf - 3, 0.0, pltpu.roll(hyst, nf - 3, 0))
        )
        for kind in range(stiff.shape[0]):
            product = jnp.dot(
                stiff[kind], nxt, precision=HIGHEST, preferred_element_type=jnp.float32
            )
            total = total - jnp.where(kinds == kind, product, 0.0)
        f_acc[:, cols] = total
        f_vel[:, cols] = v0 + 0.5 * time_step * (a0 + total)
        return carry

    def locate():
        count = route_row.shape[1]
        route = route_row[...]
        pick[...] = (
            lax.broadcasted_iota(jnp.int32, (cy, count), 0) == (site_row[...] & (cy - 1))
        ).astype(jnp.float32)
        named = (
            lax.broadcasted_iota(jnp.int32, (n_gx * n_gy, count), 0) == route
        ).astype(jnp.float32)
        earlier = (
            lax.broadcasted_iota(jnp.int32, (count, count), 0)
            < lax.broadcasted_iota(jnp.int32, (count, count), 1)
        ).astype(jnp.float32)
        ahead = jnp.dot(named, earlier, precision=HIGHEST, preferred_element_type=jnp.float32)
        rank = jnp.sum(ahead * named, axis=0, keepdims=True).astype(jnp.int32)
        owner_x = route >> (n_gy.bit_length() - 1)
        owner_y = route & (n_gy - 1)
        spot = owner_y * (n_gx * capacity) + owner_x * capacity + rank
        placing[...] = (
            lax.broadcasted_iota(jnp.int32, (slots, count), 0) == spot
        ).astype(jnp.float32)

    def parcel(axis, size, send, recv, ss, rs, off, sending):
        me = place[axis]
        to = lax.rem(me + off, size)
        source = lax.rem(me + size - off, size)
        return pltpu.make_async_remote_copy(
            src_ref=send.at[to],
            dst_ref=recv.at[me if sending else source],
            send_sem=ss.at[off], recv_sem=rs.at[off],
            device_id={axis: to}, device_id_type=MESH,
        )

    hop_1 = ("gy", n_gy, send_1, recv_1, send_1_sem, recv_1_sem)
    hop_2 = ("gx", n_gx, send_2, recv_2, send_2_sem, recv_2_sem)

    def start_hop(hop):
        axis, size, send, recv = hop[:4]
        for off in range(1, size):
            parcel(*hop, off, True).start()
        recv[place[axis]] = send[place[axis]]

    def end_hop(hop):
        for off in range(1, hop[1]):
            parcel(*hop, off, False).wait_recv()

    def post_motion():
        count = route_row.shape[1]
        cells = jnp.dot(
            ground[...].reshape(ncomp * cx, cy), pick[...],
            precision=HIGHEST, preferred_element_type=jnp.float32,
        )
        at_row = lax.broadcasted_iota(jnp.int32, (cx, count), 0) == (
            site_row[...] >> (cy.bit_length() - 1)
        )
        motion = jnp.concatenate(
            [
                jnp.sum(jnp.where(at_row, cells[c * cx:(c + 1) * cx], 0.0), axis=0, keepdims=True)
                for c in range(ncomp)
            ]
            + [jnp.zeros((8 - ncomp, count), jnp.float32)],
            axis=0,
        )
        outgoing = lax.dot_general(
            motion, placing[...], (((1,), (1,)), ((), ())),
            precision=HIGHEST, preferred_element_type=jnp.float32,
        )
        width = n_gx * capacity
        for y in range(n_gy):
            send_1[y] = outgoing[:, y * width:(y + 1) * width]
        start_hop(hop_1)

    part = n_gy * capacity
    narrow = lax.broadcasted_iota(jnp.int32, (8, LANES), 1)

    def relay_motion():
        end_hop(hop_1)
        for x in range(n_gx):
            tile, start = divmod(x * capacity, LANES)
            total = jnp.zeros((8, LANES), jnp.float32)
            for y in range(n_gy):
                piece = recv_1[y, :, tile * LANES:(tile + 1) * LANES]
                shift = (y * capacity - start) % LANES
                if shift:
                    piece = pltpu.roll(piece, shift, 1)
                here = jnp.logical_and(narrow >= y * capacity, narrow < (y + 1) * capacity)
                total = jnp.where(here, piece, total)
            send_2[x] = total
        start_hop(hop_2)

    def add_forcing():
        end_hop(hop_2)
        per_tile = LANES // part
        for tile in range(slots // LANES):
            total = recv_2[tile * per_tile]
            for i in range(1, per_tile):
                piece = pltpu.roll(recv_2[tile * per_tile + i], i * part, 1)
                total = jnp.where(narrow >= i * part, piece, total)
            moved[:, tile * LANES:(tile + 1) * LANES] = total

        def chunk(i, carry):
            cols = pl.ds(pl.multiple_of(i * LANES, LANES), LANES)
            ids = lax.broadcasted_iota(jnp.int32, (nf, LANES), 0)
            phase = ids - 3 * ((ids * 43691) >> 17)
            m = moved[:, cols]
            force = jnp.where(phase == 0, m[0:1], jnp.where(phase == 1, m[1:2], m[2:3]))
            f_acc[:, cols] = f_acc[:, cols] - force
            f_vel[:, cols] = f_vel[:, cols] - (0.5 * time_step) * force
            return carry

        lax.fori_loop(0, slots // LANES, chunk, 0)
        store(f_acc, acc_out)
        store(f_vel, vel_out)

    for c in range(ncomp):
        now_in[c].wait()
        first_edges(c, 0)
    for c in range(ncomp):
        first_edges(c, 1)
    for copy in field_in:
        copy.wait()
    top_step(0)
    for copy in frames_in:
        copy.wait()
    lax.fori_loop(0, slots // wide, frames, 0)
    store(fd, disp_out)
    store(fh, hyst_out)
    top_step(1)
    locate()
    deep_step(0, 0)
    top_step(2)
    deep_step(0, 1)
    top_step(3)
    post_motion()
    deep_step(0, 2)
    deep_step(1, 0)
    relay_motion()
    deep_step(1, 1)
    deep_step(1, 2)
    deep_step(2, 0)
    store(lev_a.at[0, pl.ds(2, nz)], before_out.at[0])
    add_forcing()
    for c in range(1, ncomp):
        deep_step(2, c)
        store(lev_a.at[c, pl.ds(2, nz)], before_out.at[c])
    for c in range(ncomp):
        deep_step(3, c)
        store(lev_b.at[c, pl.ds(2, nz)], last_out.at[c])
    for k in range(STEPS):
        for c in range(ncomp):
            for t in range(2):
                wait_sent(k, c, t)
    for hop in (hop_1, hop_2):
        for off in range(1, hop[1]):
            parcel(*hop, off, True).wait_send()
    for copy in stores:
        copy.wait()


def shards(
    n_gx, n_gy,
    u_prev, u_now, speeds, sites, routes,
    frame_disp, frame_vel, frame_acc, frame_hyst, frame_kind, stiffness,
):
    ncomp, nz, cx, cy = u_now.shape
    devices = n_gx * n_gy
    nf, slots = frame_disp.shape
    capacity = slots // devices
    count = sites.shape[0]
    f32 = jnp.float32
    i32 = jnp.int32
    field = jax.ShapeDtypeStruct(u_now.shape, f32)
    frame = jax.ShapeDtypeStruct(frame_disp.shape, f32)
    anyspec = pl.BlockSpec(memory_space=pl.ANY)
    level = pltpu.VMEM((ncomp, nz + 4, cx, cy), f32)
    x_edges = pltpu.VMEM((STEPS, ncomp, 2, nz, 2 * cy // LANES, LANES), f32)
    y_edges = pltpu.VMEM((STEPS, ncomp, 2, 2, cx, LANES), f32)
    batch = pltpu.VMEM((nf, slots), f32)
    plane = pltpu.VMEM((ncomp, cx, cy), f32)
    first_hop = pltpu.VMEM((n_gy, 8, n_gx * capacity), f32)
    second_hop = pltpu.VMEM((n_gx, 8, LANES), f32)
    halo_sem = pltpu.SemaphoreType.DMA((STEPS, ncomp, 2, 2))
    return pl.pallas_call(
        functools.partial(wave_kernel, n_gx, n_gy, capacity),
        out_shape=(field, field, frame, frame, frame, frame),
        in_specs=[anyspec] * 11,
        out_specs=(anyspec,) * 6,
        scratch_shapes=[
            level, level, pltpu.VMEM(speeds.shape, f32),
            x_edges, x_edges, y_edges, y_edges,
            batch, batch, batch, batch, pltpu.VMEM(stiffness.shape, f32), batch, batch,
            pltpu.VMEM((1, count), i32), pltpu.VMEM((1, count), i32), pltpu.VMEM((1, slots), i32),
            pltpu.VMEM((cy, count), f32), pltpu.VMEM((slots, count), f32),
            plane, plane, first_hop, first_hop, second_hop, second_hop,
            pltpu.VMEM((8, slots), f32),
            pltpu.SemaphoreType.DMA((2 * ncomp + 9,)),
            pltpu.SemaphoreType.DMA((2 * ncomp + 4,)),
            halo_sem, halo_sem, halo_sem, halo_sem,
            pltpu.SemaphoreType.DMA((n_gy,)), pltpu.SemaphoreType.DMA((n_gy,)),
            pltpu.SemaphoreType.DMA((n_gx,)), pltpu.SemaphoreType.DMA((n_gx,)),
        ],
        compiler_params=pltpu.CompilerParams(
            collective_id=0, has_side_effects=True, vmem_limit_bytes=52 * 1024 * 1024
        ),
        name="wave",
    )(
        u_prev, u_now, speeds, sites.reshape(1, count), routes.reshape(1, count),
        frame_disp, frame_vel, frame_acc, frame_hyst, frame_kind.reshape(1, slots), stiffness,
    )


def solution(mesh):
    cells = P(None, None, "gx", "gy")
    both = ("gx", "gy")
    frame = P(None, both)
    return jax.shard_map(
        functools.partial(shards, mesh.shape["gx"], mesh.shape["gy"]),
        mesh=mesh,
        in_specs=(cells, cells, cells, P(both), P(both, None), frame, frame, frame, frame,
                  P(both), P()),
        out_specs=(cells, cells, frame, frame, frame, frame),
        check_vma=False,
    )
```

time: 113 us -> 104 us (0.920)
  starting transfers between devices: 8.19 us -> 0 us
  Pallas kernels: 83.9 us -> 91.4 us
  waiting for transfers between devices: 7.41 us -> 0 us
    pallas_call x1, Pallas kernels: 81.3 us -> 91.4 us  [shards(): pl.pallas_call(functools.partial(wave_kernel, n_gx, n_gy, capacity), out_...]
    all_to_all x1 -> x0, starting transfers between devices: 8.19 us -> none  [shards(): lax.all_to_all(parcels, ('gx', 'gy'), split_axis=1, concat_axis=1, tiled=...]
    all_to_all x1 -> x0, waiting for transfers between devices: 7.41 us -> none  [shards(): lax.all_to_all(parcels, ('gx', 'gy'), split_axis=1, concat_axis=1, tiled=...]
    pallas_call x1 -> x0, Pallas kernels: 2.55 us -> none  [shards(): pl.pallas_call(forcing_kernel, grid=(slots // wide,), out_shape=(frame, f...]
    unnamed x13 -> x16, local copies, waits for them, and re-layouts: 10 us -> 11.1 us
  transfers between devices with their start and end apart: 1 -> 0, of which waited for: 1 -> 0; matrix products, arithmetic and copies ran while one was open for 0% -> 0% of each run, Pallas kernels for 0% -> 0%
where the time goes in v2:
time: 104 us
  Pallas kernels  91.4 us (88%)
  local copies, waits for them, and re-layouts  11.8 us (11%)
    pallas_call x1, Pallas kernels, shards(): pl.pallas_call(functools.partial(wave_kernel, n_gx, n_gy, capacity), out_...  91.4 us
    unnamed x16, local copies, waits for them, and re-layouts  11.1 us

profile of v2, /device:TPU:0, one launch (start us, length us, event | category | flops | bytes accessed | tf_op | source)
XLA Modules:
  0.0 103.8 jit_solution(5998557373774284049)
XLA Ops:
  0.6 0.7 reshape.21.sites
  1.3 0.0 copy-start
  1.3 0.7 copy-done
  2.0 0.0 copy-start.1
  2.0 0.7 copy-done.1
  2.7 91.4 %wave.1 = (f32[3,32,16,512]{3,2,1,0:T(8,128)}, f32[3,32,16,512]{3,2,1,0:T(8,128)}, f32[240,1024]{1,0:T(8,128)S(1)}, f32[240,1024]{1,0:T(8,128)S(1)}, f32[240,1024]{1,0:T(8,128)}, /*index=5*/f32[240,1024]{1,0:T(8,128)}) custom-call(f32[3,32,16,512]{3,2,1,0:T(8,128)} %u_prev.1, f32[3,32,16,512]{3,2,1,0:T(8,128)} %u_now.1, f32[2,32,16,512]{3,2,1,0:T(8,128)} %speeds.1, ...), custom_call_target="tpu_custom_call" | custom-call | tf_op jit(solution)/shard_map/wave/pallas_call | solution.py:471
  94.1 0.0 copy-start.2
  94.1 4.3 %copy.23 = f32[3,32,16,512]{3,2,1,0:T(8,128)} copy(f32[3,32,16,512]{3,2,1,0:T(8,128)} %get-tuple-element.12) | data formatting | bytes 6291456
  98.3 0.0 copy-done.2
  98.3 1.7 %copy.24 = f32[3,32,16,512]{3,2,1,0:T(8,128)} copy(f32[3,32,16,512]{3,2,1,0:T(8,128)S(1)} %copy-done.2) | data formatting | bytes 6291456
  100.0 0.0 copy-start.4
  100.0 0.0 copy-start.3
  100.0 0.9 copy.25
  101.0 0.9 copy.26
  101.9 0.0 copy-done.4
  101.9 0.9 copy.27
  102.8 0.0 copy-done.3
  102.8 0.9 copy.28
Async XLA Ops:
  1.3 0.7 copy-start
  2.0 0.7 copy-start.1
  94.1 4.3 %copy-start.2 = (f32[3,32,16,512]{3,2,1,0:T(8,128)S(1)}, f32[3,32,16,512]{3,2,1,0:T(8,128)}, u32[]{:S(2)}) copy-start(f32[3,32,16,512]{3,2,1,0:T(8,128)} %get-tuple-element.13) | copy-start | bytes 9437188
  100.0 1.9 %copy-start.4 = (f32[240,1024]{1,0:T(8,128)S(1)}, f32[240,1024]{1,0:T(8,128)}, u32[]{:S(2)}) copy-start(f32[240,1024]{1,0:T(8,128)} %get-tuple-element.16) | copy-start | bytes 2949124
  100.0 2.8 %copy-start.3 = (f32[240,1024]{1,0:T(8,128)S(1)}, f32[240,1024]{1,0:T(8,128)}, u32[]{:S(2)}) copy-start(f32[240,1024]{1,0:T(8,128)} %get-tuple-element.17) | copy-start | bytes 2949124

commit v3 on v2

--- a/solution.py
+++ b/solution.py
@@ -14,6 +14,7 @@
 hyst_stiff = 1.0
 ground_gain = 0.1
 LANES = 128
+GROUP = 2
 HIGHEST = lax.Precision.HIGHEST
 MESH = pl.DeviceIdType.MESH
 
@@ -139,7 +140,21 @@
 
     lane = lax.broadcasted_iota(jnp.int32, (cx, LANES), 1)
     lane_plane = lane >> 1
-    row = lax.broadcasted_iota(jnp.int32, (cx, cy), 0)
+    row = lax.broadcasted_iota(jnp.int32, (8, cy), 0)
+
+    def each_plane(low, high, body, acc):
+        whole = (high - low) // GROUP
+
+        def group(i, acc):
+            for j in range(GROUP):
+                acc = body(low + i * GROUP + j, acc)
+            return acc
+
+        if whole:
+            acc = lax.fori_loop(0, whole, group, acc)
+        for z in range(low + whole * GROUP, high):
+            acc = body(z, acc)
+        return acc
 
     def pack_edges(k, c, z, v, acc):
         head, tail = acc
@@ -152,7 +167,7 @@
                     )
         here = lane_plane == z
         head = jnp.where(here, pltpu.roll(v[:, :LANES], 2 * z, 1), head)
-        tail = jnp.where(here, pltpu.roll(v[:, cy - LANES:], lax.rem(2 * z + 2, LANES), 1), tail)
+        tail = jnp.where(here, pltpu.roll(v[:, cy - LANES:], (2 * z + 2) % LANES, 1), tail)
         return head, tail
 
     blank = (jnp.zeros((cx, LANES), jnp.float32),) * 2
@@ -173,10 +188,22 @@
                 )
 
             xl0, xl1, xr0, xr1 = edge(0, 0), edge(0, 1), edge(1, 0), edge(1, 1)
-            w1 = jnp.where(row == 0, xl1, pltpu.roll(u, 1, 0))
-            w2 = jnp.where(row == 0, xl0, jnp.where(row == 1, xl1, pltpu.roll(u, 2, 0)))
-            e1 = jnp.where(row == cx - 1, xr0, pltpu.roll(u, cx - 1, 0))
-            e2 = jnp.where(row == cx - 2, xr0, jnp.where(row == cx - 1, xr1, pltpu.roll(u, cx - 2, 0)))
+            def upper(values, *fixes):
+                rim = values[:8]
+                for at, fix in fixes:
+                    rim = jnp.where(row == at, fix, rim)
+                return jnp.concatenate([rim, values[8:]], axis=0)
+
+            def lower(values, *fixes):
+                rim = values[cx - 8:]
+                for at, fix in fixes:
+                    rim = jnp.where(row == at, fix, rim)
+                return jnp.concatenate([values[:cx - 8], rim], axis=0)
+
+            w1 = upper(pltpu.roll(u, 1, 0), (0, xl1))
+            w2 = upper(pltpu.roll(u, 2, 0), (0, xl0), (1, xl1))
+            e1 = lower(pltpu.roll(u, cx - 1, 0), (7, xr0))
+            e2 = lower(pltpu.roll(u, cx - 2, 0), (6, xr0), (7, xr1))
             east = 16.0 * (w1 + e1) - (w2 + e2)
             yl = yrecv[k, c, t, 0]
             yr = yrecv[k, c, t, 1]
@@ -197,7 +224,7 @@
 
             back = LANES - 1 - 2 * z
             s1 = first(pltpu.roll(u, 1, 1), 1, pltpu.roll(yl, back, 1))
-            s2 = first(pltpu.roll(u, 2, 1), 2, pltpu.roll(yl, lax.rem(back + 1, LANES), 1))
+            s2 = first(pltpu.roll(u, 2, 1), 2, pltpu.roll(yl, (back + 1) % LANES, 1))
             n1 = final(pltpu.roll(u, cy - 1, 1), 1, pltpu.roll(yr, back, 1))
             n2 = final(pltpu.roll(u, cy - 2, 1), 2, pltpu.roll(yr, back - 1, 1))
             north = 16.0 * (s1 + n1) - (s2 + n2)
@@ -210,7 +237,7 @@
                 return pack_edges(k + 1, c, z, v, acc)
             return acc
 
-        return lax.fori_loop(low, high, plane, acc)
+        return each_plane(low, high, plane, acc)
 
     def levels(k):
         return (lev_a, lev_b) if k % 2 == 0 else (lev_b, lev_a)
@@ -246,7 +273,7 @@
 
     def first_edges(c, t):
         low, high = planes(0, t)
-        acc = lax.fori_loop(
+        acc = each_plane(
             low, high, lambda z, acc: pack_edges(0, c, z, lev_b[c, z + 2], acc), blank
         )
         put_y(0, c, t, acc)

time: 104 us -> 98.4 us (0.946)
  the two profiles are of different devices: /device:TPU:0 before, /device:TPU:14 now
where the time goes in v3:
time: 98.4 us; the launch traced here: 98.2 us
  Pallas kernels  85.8 us (87%)
  local copies, waits for them, and re-layouts  11.8 us (12%)
    pallas_call x1, Pallas kernels, shards(): pl.pallas_call(functools.partial(wave_kernel, n_gx, n_gy, capacity), out_...  85.8 us
    unnamed x16, local copies, waits for them, and re-layouts  11.1 us

profile of v3, /device:TPU:14, one launch (start us, length us, event | category | flops | bytes accessed | tf_op | source)
XLA Modules:
  0.0 98.2 jit_solution(14353018680243835438)
XLA Ops:
  0.6 0.7 reshape.21.sites
  1.3 0.0 copy-start
  1.3 0.7 copy-done
  2.0 0.0 copy-start.1
  2.0 0.7 copy-done.1
  2.7 85.8 %wave.1 = (f32[3,32,16,512]{3,2,1,0:T(8,128)}, f32[3,32,16,512]{3,2,1,0:T(8,128)}, f32[240,1024]{1,0:T(8,128)S(1)}, f32[240,1024]{1,0:T(8,128)S(1)}, f32[240,1024]{1,0:T(8,128)}, /*index=5*/f32[240,1024]{1,0:T(8,128)}) custom-call(f32[3,32,16,512]{3,2,1,0:T(8,128)} %u_prev.1, f32[3,32,16,512]{3,2,1,0:T(8,128)} %u_now.1, f32[2,32,16,512]{3,2,1,0:T(8,128)} %speeds.1, ...), custom_call_target="tpu_custom_call" | custom-call | tf_op jit(solution)/shard_map/wave/pallas_call | solution.py:498
  88.5 0.0 copy-start.2
  88.5 4.3 %copy.23 = f32[3,32,16,512]{3,2,1,0:T(8,128)} copy(f32[3,32,16,512]{3,2,1,0:T(8,128)} %get-tuple-element.12) | data formatting | bytes 6291456
  92.7 0.0 copy-done.2
  92.8 1.7 %copy.24 = f32[3,32,16,512]{3,2,1,0:T(8,128)} copy(f32[3,32,16,512]{3,2,1,0:T(8,128)S(1)} %copy-done.2) | data formatting | bytes 6291456
  94.4 0.0 copy-start.4
  94.4 0.0 copy-start.3
  94.4 0.9 copy.25
  95.4 0.9 copy.26
  96.3 0.0 copy-done.4
  96.3 0.9 copy.27
  97.3 0.0 copy-done.3
  97.3 0.9 copy.28
Async XLA Ops:
  1.3 0.7 copy-start
  2.0 0.7 copy-start.1
  88.5 4.3 %copy-start.2 = (f32[3,32,16,512]{3,2,1,0:T(8,128)S(1)}, f32[3,32,16,512]{3,2,1,0:T(8,128)}, u32[]{:S(2)}) copy-start(f32[3,32,16,512]{3,2,1,0:T(8,128)} %get-tuple-element.13) | copy-start | bytes 9437188
  94.4 1.9 %copy-start.4 = (f32[240,1024]{1,0:T(8,128)S(1)}, f32[240,1024]{1,0:T(8,128)}, u32[]{:S(2)}) copy-start(f32[240,1024]{1,0:T(8,128)} %get-tuple-element.16) | copy-start | bytes 2949124
  94.4 2.8 %copy-start.3 = (f32[240,1024]{1,0:T(8,128)S(1)}, f32[240,1024]{1,0:T(8,128)}, u32[]{:S(2)}) copy-start(f32[240,1024]{1,0:T(8,128)} %get-tuple-element.17) | copy-start | bytes 2949124
